TPU v7x, 32 devices: a whole 2x2x4 slice. The times are simulated.
32 devices in a mesh: groups: 1, col: 8 (over y, x, core), row: 4 (over z).
Axes of the slice: x: 2, y: 2, z: 4, core: 2. Of those that a mesh axis runs over, the one named last changes fastest.
Arguments:
- features: bfloat16 [16384, 128], P(('groups', 'row', 'col')), may hold values from -6 to 6
- adjacency: bfloat16 [256, 64, 5632], P(('groups', 'col'), None, 'row'), may hold values from -0.125 to 0.125
- tile_cols: int32 [256, 88], P(('groups', 'col'), 'row'), may hold values from 0 to 63
- row_counts: int32 [256, 4], P(('groups', 'col'), 'row'), may hold values from 1 to 22, as said below
- weight: bfloat16 [128, 128], replicated, may hold values from -0.5 to 0.5
- bias: float32 [128], replicated, may hold values from -3 to 3
- out_grad: bfloat16 [16384, 128], P(('groups', 'col', 'row')), may hold values from -6 to 6
Outputs:
- activations: bfloat16 [16384, 128], P(('groups', 'col', 'row'))
- feature_grad: bfloat16 [16384, 128], P(('groups', 'row', 'col'))
- weight_grad: float32 [128, 128], P('groups')
- bias_grad: float32 [128], P('groups')
Inputs may be any that keep to these rules, and one draw needn't show every extreme that they name: `row_counts`: live slots of a block row come first among its 22 slots on each row index; at least one entry equals 22. `tile_cols`: block column within the source range of row index s // 22.
All inputs are finite; a program needn't handle non-finite values.
Results may differ from a plain program's by a relative error of at most 0.006.
Values may be sent and summed in bfloat16 or wider, within the bound.
A program may use at most 128 MiB of HBM per device.

v0:
```python
import functools
import math

import jax
import jax.numpy as jnp
from jax import lax
from jax.experimental import pallas as pl
from jax.experimental.pallas import tpu as pltpu
from jax.sharding import PartitionSpec as P

MESH = pl.DeviceIdType.MESH
F32, BF16 = jnp.float32, jnp.bfloat16
MIB = 1024 * 1024


def col_peers(nc):
    c = lax.axis_index("col")
    outer, core, n_out = c // 2, c % 2, nc // 2
    partner = outer * 2 + (1 - core)
    ahead = [lax.rem(outer + d, n_out) * 2 + core for d in range(n_out)]
    behind = [lax.rem(outer - d + n_out, n_out) * 2 + core for d in range(n_out)]
    return c, partner, ahead, behind


def send(src, dst, send_sem, recv_sem, where):
    return pltpu.make_async_remote_copy(
        src_ref=src, dst_ref=dst, send_sem=send_sem, recv_sem=recv_sem,
        device_id=where, device_id_type=MESH,
    )


def forward_kernel(
    nc, nr, scale, idx_ref, feat_ref, adj_hbm, weight_ref, bias_ref, og_ref,
    act_ref, grads_ref, wb_ref,
    xg, adj, xs, own, part, rbuf, gg,
    a_sem, f_send, f_recv, p_send, p_recv, r_send, r_recv, g_send, g_recv,
):
    blocks, tile, slot_width = adj.shape
    per_row = slot_width // tile
    chunk = blocks // nr
    rows = chunk * tile
    n_out = nc // 2
    own_blocks = feat_ref.shape[0] // tile
    c, partner, ahead, behind = col_peers(nc)
    r = lax.axis_index("row")
    row_at = [lax.rem(r + e, nr) for e in range(nr)]

    loads = []
    for e in range(nr):
        t = row_at[(e + 1) % nr]
        cut = pl.ds(t * chunk, chunk)
        load = pltpu.make_async_copy(adj_hbm.at[cut], adj.at[cut], a_sem.at[e])
        load.start()
        loads.append(load)

    barrier = pltpu.get_barrier_semaphore()
    pl.semaphore_signal(barrier, inc=1, device_id={"col": partner}, device_id_type=MESH)
    for d in range(1, n_out):
        pl.semaphore_signal(barrier, inc=1, device_id={"col": ahead[d]}, device_id_type=MESH)
    for e in range(1, nr):
        pl.semaphore_signal(barrier, inc=1, device_id={"row": row_at[e]}, device_id_type=MESH)

    def blocks_of(col):
        return xg.at[pl.ds(col * own_blocks, own_blocks)]

    xg[pl.ds(c * own_blocks, own_blocks)] = feat_ref[...].reshape(own_blocks, tile, -1)
    xg[nc * own_blocks] = jnp.zeros(xg.shape[1:], xg.dtype)
    pl.semaphore_wait(barrier, 1 + (n_out - 1) + (nr - 1))

    copies = []
    for d in range(1, n_out):
        copy = send(blocks_of(c), blocks_of(c), f_send.at[d], f_recv.at[d], {"col": ahead[d]})
        copy.start()
        copies.append(copy)
    pair = []
    copy = send(blocks_of(c), blocks_of(c), p_send.at[0], p_recv.at[0], {"col": partner})
    copy.start()
    pair.append(copy)
    for d in range(1, n_out):
        copies[d - 1].wait_recv()
        came = blocks_of(behind[d])
        copy = send(came, came, p_send.at[d], p_recv.at[d], {"col": partner})
        copy.start()
        pair.append(copy)
    for copy in pair:
        copy.wait_recv()
    for copy in copies + pair:
        copy.wait_send()

    row_copies = []
    for e in range(nr):
        far = (e + 1) % nr
        t = row_at[far]
        loads[e].wait()

        def block_row(i, carry, t=t, far=far):
            b = t * chunk + i
            for s in range(per_row):
                xs[pl.ds(s * tile, tile)] = xg[idx_ref[b * per_row + s]]
            got = jnp.dot(adj[b], xs[...], preferred_element_type=F32)
            cut = pl.ds(pl.multiple_of(i * tile, tile), tile)
            if far:
                part[far - 1, cut, :] = got.astype(BF16)
            else:
                own[cut, :] = got
            return carry

        lax.fori_loop(0, chunk, block_row, 0)
        if far:
            copy = send(
                part.at[far - 1], rbuf.at[far - 1], r_send.at[far - 1], r_recv.at[far - 1], {"row": t}
            )
            copy.start()
            row_copies.append(copy)
    summed = own[...]
    for copy in row_copies:
        copy.wait_recv()
    for e in range(nr - 1):
        summed = summed + rbuf[e].astype(F32)
    hidden = summed.astype(BF16)
    preact = jnp.dot(hidden, weight_ref[...], preferred_element_type=F32) + bias_ref[...]
    sig = jax.nn.sigmoid(preact)
    pre_grad = og_ref[...].astype(F32) * (sig * (1.0 + preact * (1.0 - sig)))
    half = pre_grad.astype(BF16)
    dest = lax.dot_general(
        half, weight_ref[...], (((1,), (1,)), ((), ())), preferred_element_type=F32
    )
    gg[r] = dest.astype(BF16)
    grad_copies = []
    for e in range(1, nr):
        copy = send(gg.at[r], gg.at[r], g_send.at[e - 1], g_recv.at[e - 1], {"row": row_at[e]})
        copy.start()
        grad_copies.append(copy)
    act_ref[...] = (preact * sig).astype(BF16)
    wb_ref[pl.ds(0, hidden.shape[1]), :] = scale * lax.dot_general(
        hidden, half, (((0,), (0,)), ((), ())), preferred_element_type=F32
    )
    wb_ref[pl.ds(hidden.shape[1], 8), :] = jnp.broadcast_to(
        scale * jnp.sum(pre_grad, axis=0, keepdims=True), (8, hidden.shape[1])
    )
    for copy in grad_copies:
        copy.wait_recv()
    grads_ref[...] = gg[...].reshape(grads_ref.shape)
    for copy in row_copies + grad_copies:
        copy.wait_send()


def backward_kernel(group, idx_ref, adj_ref, grad_ref, out_ref, *accs):
    step = pl.program_id(0)
    unused, tile, slot_width = adj_ref.shape
    per_row = slot_width // tile

    @pl.when(step == 0)
    def start():
        for acc in accs:
            acc[...] = jnp.zeros_like(acc)

    def block_row(i, carry):
        b = step * group + i
        contrib = lax.dot_general(
            adj_ref[i], grad_ref[pl.ds(pl.multiple_of(i * tile, tile), tile), :],
            (((0,), (0,)), ((), ())), preferred_element_type=F32,
        )
        for s in range(per_row):
            acc = accs[s % len(accs)]
            j = idx_ref[b * per_row + s]
            acc[j] = acc[j] + contrib[s * tile : (s + 1) * tile]
        return carry

    lax.fori_loop(0, group, block_row, 0)

    @pl.when(step == pl.num_programs(0) - 1)
    def finish():
        n = out_ref.shape[0]
        total = accs[0][pl.ds(0, n)]
        for acc in accs[1:]:
            total = total + acc[pl.ds(0, n)]
        out_ref[...] = total.astype(BF16)


def scatter_kernel(nc, part_ref, out_ref, from_pair, send_buf, from_chip, p_send, p_recv, s_send, s_recv):
    n_out = nc // 2
    c, partner, ahead, behind = col_peers(nc)
    partner_ahead = [x + partner - c for x in ahead]
    barrier = pltpu.get_barrier_semaphore()
    pl.semaphore_signal(barrier, inc=1, device_id={"col": partner}, device_id_type=MESH)
    for d in range(1, n_out):
        pl.semaphore_signal(barrier, inc=1, device_id={"col": ahead[d]}, device_id_type=MESH)
    pl.semaphore_wait(barrier, n_out)
    order = list(range(1, n_out)) + [0]
    pair = {}
    for d in order:
        pair[d] = send(
            part_ref.at[partner_ahead[d]], from_pair.at[d], p_send.at[d], p_recv.at[d], {"col": partner}
        )
        pair[d].start()
    copies = []
    for d in order:
        pair[d].wait_recv()
        both = part_ref[ahead[d]].astype(F32) + from_pair[d].astype(F32)
        if d:
            send_buf[d - 1] = both.astype(BF16)
            copy = send(
                send_buf.at[d - 1], from_chip.at[d - 1], s_send.at[d - 1], s_recv.at[d - 1], {"col": ahead[d]}
            )
            copy.start()
            copies.append(copy)
    for d in range(1, n_out):
        copies[d - 1].wait_recv()
        both = both + from_chip[d - 1].astype(F32)
    out_ref[...] = both.astype(BF16)
    for copy in copies + [pair[d] for d in order]:
        copy.wait_send()


def on_device(mesh, features, adjacency, tile_cols, row_counts, weight, bias, out_grad):
    blocks, tile, slot_width = adjacency.shape
    per_row = slot_width // tile
    own_rows, feat = features.shape
    nc, nr = mesh.shape["col"], mesh.shape["row"]
    n_out = nc // 2
    col_blocks = nc * own_rows // tile
    scale = 1.0 / math.sqrt(own_rows * nc * nr)
    live = jnp.arange(per_row, dtype=jnp.int32)[None, :] < row_counts
    idx = jnp.where(live, tile_cols, col_blocks).reshape(-1)

    vmem = pl.BlockSpec(memory_space=pltpu.VMEM)
    smem = pl.BlockSpec(memory_space=pltpu.SMEM)
    hbm = pl.BlockSpec(memory_space=pl.ANY)
    dma = pltpu.SemaphoreType.DMA
    rows = blocks * tile // nr
    tile_flops = 2 * blocks * tile * slot_width * feat
    activations, grads, wb = pl.pallas_call(
        functools.partial(forward_kernel, nc, nr, scale),
        out_shape=(
            jax.ShapeDtypeStruct((rows, feat), BF16),
            jax.ShapeDtypeStruct((blocks * tile, feat), BF16),
            jax.ShapeDtypeStruct((feat + 8, feat), F32),
        ),
        in_specs=[smem, vmem, hbm, vmem, vmem, vmem],
        out_specs=(vmem, vmem, vmem),
        scratch_shapes=[
            pltpu.VMEM((col_blocks + 1, tile, feat), BF16),
            pltpu.VMEM((blocks, tile, slot_width), BF16),
            pltpu.VMEM((slot_width, feat), BF16),
            pltpu.VMEM((rows, feat), F32),
            pltpu.VMEM((nr - 1, rows, feat), BF16),
            pltpu.VMEM((nr - 1, rows, feat), BF16),
            pltpu.VMEM((nr, rows, feat), BF16),
            dma((nr,)), dma((n_out,)), dma((n_out,)), dma((n_out,)), dma((n_out,)),
            dma((nr - 1,)), dma((nr - 1,)), dma((nr - 1,)), dma((nr - 1,)),
        ],
        compiler_params=pltpu.CompilerParams(
            collective_id=0, has_side_effects=True, vmem_limit_bytes=40 * MIB
        ),
        cost_estimate=pl.CostEstimate(
            flops=tile_flops, bytes_accessed=adjacency.size * 2, transcendentals=rows * feat
        ),
    )(idx, features, adjacency, weight, bias.reshape(1, -1), out_grad)

    wb = lax.psum(wb, ("col", "row"))

    group = math.gcd(blocks, 4)
    partial = pl.pallas_call(
        functools.partial(backward_kernel, group),
        grid=(blocks // group,),
        out_shape=jax.ShapeDtypeStruct((col_blocks, tile, feat), BF16),
        in_specs=[
            smem,
            pl.BlockSpec((group, tile, slot_width), lambda i: (i, 0, 0)),
            pl.BlockSpec((group * tile, feat), lambda i: (i, 0)),
        ],
        out_specs=pl.BlockSpec((col_blocks, tile, feat), lambda i: (0, 0, 0)),
        scratch_shapes=[pltpu.VMEM((col_blocks + 1, tile, feat), F32) for unused in range(2)],
        compiler_params=pltpu.CompilerParams(vmem_limit_bytes=40 * MIB),
        cost_estimate=pl.CostEstimate(
            flops=tile_flops * 8, bytes_accessed=adjacency.size * 2, transcendentals=0
        ),
    )(idx, adjacency, grads)

    feature_grad = pl.pallas_call(
        functools.partial(scatter_kernel, nc),
        out_shape=jax.ShapeDtypeStruct((own_rows, feat), BF16),
        in_specs=[vmem],
        out_specs=vmem,
        scratch_shapes=[
            pltpu.VMEM((n_out, own_rows, feat), BF16),
            pltpu.VMEM((n_out - 1, own_rows, feat), BF16),
            pltpu.VMEM((n_out - 1, own_rows, feat), BF16),
            dma((n_out,)), dma((n_out,)), dma((n_out - 1,)), dma((n_out - 1,)),
        ],
        compiler_params=pltpu.CompilerParams(
            collective_id=1, has_side_effects=True, vmem_limit_bytes=20 * MIB
        ),
        cost_estimate=pl.CostEstimate(
            flops=own_rows * nc * feat, bytes_accessed=8 * own_rows * nc * feat, transcendentals=0
        ),
    )(partial.reshape(nc, own_rows, feat))
    return (activations, feature_grad, wb[:feat], wb[feat])


def solution(mesh):
    placed = (
        P(("groups", "row", "col"), None),
        P(("groups", "col"), None, "row"),
        P(("groups", "col"), "row"),
        P(("groups", "col"), "row"),
        P(),
        P(),
        P(("groups", "col", "row"), None),
    )
    return jax.shard_map(
        functools.partial(on_device, mesh),
        mesh=mesh,
        in_specs=placed,
        out_specs=(
            P(("groups", "col", "row"), None),
            P(("groups", "row", "col"), None),
            P("groups", None),
            P("groups"),
        ),
        check_vma=False,
    )
```

profile of v0, /device:TPU:0, one launch (start us, length us, event | category | flops | bytes accessed | tf_op | source)
XLA Modules:
  0.0 187.8 jit_solution(12610453681884475909)
XLA Ops:
  7.2 0.0 all-reduce.2.cloned.1.call-start
  7.2 0.7 fusion
  7.9 0.1 copy.11
  8.0 0.1 reshape.17.idx_ref
  8.1 0.0 copy-start
  8.1 2.6 %copy-done = bf16[32,64,1408]{2,1,0:T(8,128)(2,1)S(1)} copy-done((bf16[32,64,1408]{2,1,0:T(8,128)(2,1)S(1)}, bf16[32,64,1408]{2,1,0:T(8,128)(2,1)}, u32[]{:S(2)}) %copy-start) | copy-done | bytes 5767192
  10.8 0.0 copy-start.2
  10.8 0.9 copy-done.2
  11.7 0.0 copy-start.3
  11.7 0.9 copy-done.3
  12.6 0.0 copy-start.4
  12.6 0.8 copy-done.4
  13.3 0.0 copy-start.5
  13.3 0.7 copy-done.5
  14.0 40.5 %shard_map.102 = (bf16[512,128]{1,0:T(8,128)(2,1)S(1)}, bf16[2048,128]{1,0:T(8,128)(2,1)S(1)}, f32[136,128]{1,0:T(8,128)}) custom-call(s32[704]{0:T(1024)S(1)} %reshape.17.idx_ref, bf16[512,128]{1,0:T(8,128)(2,1)S(1)} %copy-done.2, bf16[32,64,1408]{2,1,0:T(8,128)(2,1)S(1)} %copy-done, bf16[128,128]{1,0:T(8,128)(2,1)S(1)} %copy-done.4, f32[1,128]{1,0:T(1,128)S(1)} %bitcast.6, ...), custom_call_target="tpu_custom_call" | custom-call | flops 738197504 | bytes 5767168 | tf_op jit(solution)/shard_map/pallas_call | solution.py:233
  54.5 0.0 all-reduce.2.cloned.1.call-update
  54.5 0.0 copy-start.1
  54.6 2.6 %copy-done.1 = bf16[32,64,1408]{2,1,0:T(8,128)(2,1)S(1)} copy-done((bf16[32,64,1408]{2,1,0:T(8,128)(2,1)S(1)}, bf16[32,64,1408]{2,1,0:T(8,128)(2,1)}, u32[]{:S(2)}) %copy-start.1) | copy-done | bytes 5767192
  57.2 11.5 %shard_map.103 = bf16[64,64,128]{2,1,0:T(8,128)(2,1)S(1)} custom-call(s32[704]{0:T(1024)S(1)} %reshape.17.idx_ref, bf16[32,64,1408]{2,1,0:T(8,128)(2,1)S(1)} %copy-done.1, bf16[2048,128]{1,0:T(8,128)(2,1)S(1)} %get-tuple-element.8.grad_ref), custom_call_target="tpu_custom_call" | custom-call | flops 5905580032 | bytes 5767168 | tf_op jit(solution)/shard_map/pallas_call | solution.py:264
  68.7 11.1 %shard_map.104 = bf16[512,128]{1,0:T(8,128)(2,1)S(1)} custom-call(bf16[8,512,128]{2,1,0:T(8,128)(2,1)S(1)} %bitcast.5), custom_call_target="tpu_custom_call" | custom-call | flops 524288 | bytes 4194304 | tf_op jit(solution)/shard_map/pallas_call | solution.py:281
  79.8 97.2 %all-reduce.2.cloned.1.call-done = f32[136,128]{1,0:T(8,128)} async-done(((f32[136,128]{1,0:T(8,128)}), f32[136,128]{1,0:T(8,128)}) %all-reduce.2.cloned.1.call-update) | async-done | bytes 69648 | tf_op jit(solution)/shard_map/psum | solution.py:261
  177.0 1.2 slice_bitcast_fusion
  178.2 1.5 slice.8
  179.7 0.7 copy.15
  180.3 0.7 copy.16
Async XLA Ops:
  7.2 169.8 %all-reduce.2.cloned.1.call-start = ((), (), s32[]{:S(2)}) async-start(), calls=%async_computation | async-start | bytes 139264 | tf_op jit(solution)/shard_map/psum | solution.py:261
  8.1 2.6 %copy-start = (bf16[32,64,1408]{2,1,0:T(8,128)(2,1)S(1)}, bf16[32,64,1408]{2,1,0:T(8,128)(2,1)}, u32[]{:S(2)}) copy-start(bf16[32,64,1408]{2,1,0:T(8,128)(2,1)} %adj_ref.1) | copy-start | bytes 17301508
  10.8 0.9 copy-start.2
  11.7 0.9 copy-start.3
  12.6 0.8 copy-start.4
  13.3 0.7 copy-start.5
  54.5 2.6 %copy-start.1 = (bf16[32,64,1408]{2,1,0:T(8,128)(2,1)S(1)}, bf16[32,64,1408]{2,1,0:T(8,128)(2,1)}, u32[]{:S(2)}) copy-start(bf16[32,64,1408]{2,1,0:T(8,128)(2,1)} %adj_ref.1) | copy-start | bytes 17301508
Sparse Core Ops, SparseCore 0:
  54.7 122.3 all-reduce.1
where the time goes:
time: 189 us; the launch traced here: 188 us
  waiting for transfers between devices  97.2 us (51%)
  Pallas kernels  63.1 us (33%)
  between operations  14.1 us (7%)
  local copies, waits for them, and re-layouts  12.6 us (7%)
    psum x1, waiting for transfers between devices, on_device(): wb = lax.psum(wb, ('col', 'row'))  97.2 us
    pallas_call x1, Pallas kernels, on_device(): pl.pallas_call(functools.partial(forward_kernel, nc, nr, scale), out_shap...  40.5 us
    pallas_call x1, Pallas kernels, on_device(): pl.pallas_call(functools.partial(backward_kernel, group), grid=(blocks //...  11.5 us
    pallas_call x1, Pallas kernels, on_device(): pl.pallas_call(functools.partial(scatter_kernel, nc), out_shape=jax.Shape...  11.1 us
    unnamed x14, local copies, waits for them, and re-layouts  9.79 us
  transfers between devices with their start and end apart: 1, of which 1 were waited for; matrix products, arithmetic and copies ran while one was open for 0% of the time, Pallas kernels for 12%

commit v1 on v0

v1 whole, which is shorter than its diff:
```python
import functools
import math

import jax
import jax.numpy as jnp
from jax import lax
from jax.experimental import pallas as pl
from jax.experimental.pallas import tpu as pltpu
from jax.sharding import PartitionSpec as P

MESH = pl.DeviceIdType.MESH
F32, BF16 = jnp.float32, jnp.bfloat16
MIB = 1024 * 1024


def col_peers(nc):
    c = lax.axis_index("col")
    outer, core, n_out = c // 2, c % 2, nc // 2
    partner = outer * 2 + (1 - core)
    ahead = [lax.rem(outer + d, n_out) * 2 + core for d in range(n_out)]
    behind = [lax.rem(outer - d + n_out, n_out) * 2 + core for d in range(n_out)]
    return c, partner, ahead, behind


def send(src, dst, send_sem, recv_sem, where):
    return pltpu.make_async_remote_copy(
        src_ref=src, dst_ref=dst, send_sem=send_sem, recv_sem=recv_sem,
        device_id=where, device_id_type=MESH,
    )


def forward_kernel(
    nc, nr, scale, cols_ref, counts_ref, feat_hbm, adj_hbm, weight_hbm, bias_hbm, og_hbm,
    act_ref, grads_ref, wb_ref,
    xg, adj, weight_ref, bias_ref, og_ref, own, part, rbuf, gg,
    in_sem, a_sem, f_send, f_recv, p_send, p_recv, r_send, r_recv, g_send, g_recv,
):
    blocks, tile, slot_width = adj.shape
    per_row = slot_width // tile
    chunk = blocks // nr
    rows = chunk * tile
    n_out = nc // 2
    own_blocks = feat_hbm.shape[0]
    c, partner, ahead, behind = col_peers(nc)
    r = lax.axis_index("row")
    row_at = [lax.rem(r + e, nr) for e in range(nr)]

    mine = xg.at[pl.ds(c * own_blocks, own_blocks)]
    first = pltpu.make_async_copy(feat_hbm, mine, in_sem.at[0])
    first.start()
    loads = []
    for e in range(nr):
        t = row_at[(e + 1) % nr]
        cut = pl.ds(t * chunk, chunk)
        load = pltpu.make_async_copy(adj_hbm.at[cut], adj.at[cut], a_sem.at[e])
        load.start()
        loads.append(load)
    small = []
    for n, (src, dst) in enumerate(((weight_hbm, weight_ref), (bias_hbm, bias_ref), (og_hbm, og_ref))):
        load = pltpu.make_async_copy(src, dst, in_sem.at[n + 1])
        load.start()
        small.append(load)

    barrier = pltpu.get_barrier_semaphore()
    pl.semaphore_signal(barrier, inc=1, device_id={"col": partner}, device_id_type=MESH)
    for d in range(1, n_out):
        pl.semaphore_signal(barrier, inc=1, device_id={"col": ahead[d]}, device_id_type=MESH)
    for e in range(1, nr):
        pl.semaphore_signal(barrier, inc=1, device_id={"row": row_at[e]}, device_id_type=MESH)

    def blocks_of(col):
        return xg.at[pl.ds(col * own_blocks, own_blocks)]

    xg[nc * own_blocks] = jnp.zeros(xg.shape[1:], xg.dtype)
    first.wait()
    pl.semaphore_wait(barrier, 1 + (n_out - 1) + (nr - 1))

    copies = []
    for d in range(1, n_out):
        copy = send(blocks_of(c), blocks_of(c), f_send.at[d], f_recv.at[d], {"col": ahead[d]})
        copy.start()
        copies.append(copy)
    pair = []
    copy = send(blocks_of(c), blocks_of(c), p_send.at[0], p_recv.at[0], {"col": partner})
    copy.start()
    pair.append(copy)
    for d in range(1, n_out):
        copies[d - 1].wait_recv()
        came = blocks_of(behind[d])
        copy = send(came, came, p_send.at[d], p_recv.at[d], {"col": partner})
        copy.start()
        pair.append(copy)
    for copy in pair:
        copy.wait_recv()
    for copy in copies + pair:
        copy.wait_send()

    row_copies = []
    for e in range(nr):
        far = (e + 1) % nr
        t = row_at[far]
        loads[e].wait()

        def block_row(i, carry, t=t, far=far):
            b = t * chunk + i
            count = counts_ref[b, 0]
            picked = [
                xg[jnp.where(s < count, cols_ref[b, s], nc * own_blocks)] for s in range(per_row)
            ]
            got = jnp.dot(adj[b], jnp.concatenate(picked, axis=0), preferred_element_type=F32)
            cut = pl.ds(pl.multiple_of(i * tile, tile), tile)
            if far:
                part[far - 1, cut, :] = got.astype(BF16)
            else:
                own[cut, :] = got
            return carry

        lax.fori_loop(0, chunk, block_row, 0)
        if far:
            copy = send(
                part.at[far - 1], rbuf.at[far - 1], r_send.at[far - 1], r_recv.at[far - 1], {"row": t}
            )
            copy.start()
            row_copies.append(copy)
    summed = own[...]
    for copy in row_copies:
        copy.wait_recv()
    for e in range(nr - 1):
        summed = summed + rbuf[e].astype(F32)
    hidden = summed.astype(BF16)
    for load in small:
        load.wait()
    preact = jnp.dot(hidden, weight_ref[...], preferred_element_type=F32) + bias_ref[...]
    sig = jax.nn.sigmoid(preact)
    pre_grad = og_ref[...].astype(F32) * (sig * (1.0 + preact * (1.0 - sig)))
    half = pre_grad.astype(BF16)
    dest = lax.dot_general(
        half, weight_ref[...], (((1,), (1,)), ((), ())), preferred_element_type=F32
    )
    gg[r] = dest.astype(BF16)
    grad_copies = []
    for e in range(1, nr):
        copy = send(gg.at[r], gg.at[r], g_send.at[e - 1], g_recv.at[e - 1], {"row": row_at[e]})
        copy.start()
        grad_copies.append(copy)
    act_ref[...] = (preact * sig).astype(BF16)
    feat = hidden.shape[1]
    cut = feat // nr
    wb_ref[:, pl.ds(0, cut), :] = scale * lax.dot_general(
        hidden, half, (((0,), (0,)), ((), ())), preferred_element_type=F32
    ).reshape(nr, cut, feat)
    wb_ref[:, pl.ds(cut, 8), :] = jnp.broadcast_to(
        scale * jnp.sum(pre_grad, axis=0, keepdims=True), (nr, 8, feat)
    )
    for copy in grad_copies:
        copy.wait_recv()
    grads_ref[...] = gg[...].reshape(grads_ref.shape)
    for copy in row_copies + grad_copies:
        copy.wait_send()


def backward_kernel(group, cols_ref, counts_ref, adj_hbm, grad_ref, out_ref, adj, a_sem, *accs):
    blocks, tile, slot_width = adj.shape
    per_row = slot_width // tile
    dead = out_ref.shape[0]

    def load(g):
        cut = pl.ds(g * group, group)
        return pltpu.make_async_copy(adj_hbm.at[cut], adj.at[cut], a_sem.at[g])

    for g in range(blocks // group):
        load(g).start()
    for acc in accs:
        acc[...] = jnp.zeros_like(acc)

    def block_row(i, g):
        b = g * group + i
        contrib = lax.dot_general(
            adj[b], grad_ref[pl.ds(pl.multiple_of(b * tile, tile), tile), :],
            (((0,), (0,)), ((), ())), preferred_element_type=F32,
        )
        count = counts_ref[b, 0]
        for s in range(per_row):
            acc = accs[s % len(accs)]
            j = jnp.where(s < count, cols_ref[b, s], dead)
            acc[j] = acc[j] + contrib[s * tile : (s + 1) * tile]
        return g

    def block_rows(g, carry):
        load(g).wait()
        lax.fori_loop(0, group, block_row, g)
        return carry

    lax.fori_loop(0, blocks // group, block_rows, 0)
    total = accs[0][pl.ds(0, dead)]
    for acc in accs[1:]:
        total = total + acc[pl.ds(0, dead)]
    out_ref[...] = total.astype(BF16)


def scatter_kernel(
    nc, nr, part_ref, wb_ref, out_ref, wg_ref, bg_ref,
    from_pair, send_buf, from_chip, w_row, w_sum, w_pair, w_chip, w_all,
    p_send, p_recv, s_send, s_recv, wr_send, wr_recv, wp_send, wp_recv, wc_send, wc_recv, wa_send, wa_recv,
):
    n_out = nc // 2
    c, partner, ahead, behind = col_peers(nc)
    outer = c // 2
    r = lax.axis_index("row")
    row_at = [lax.rem(r + e, nr) for e in range(nr)]
    partner_ahead = [x + partner - c for x in ahead]
    barrier = pltpu.get_barrier_semaphore()
    pl.semaphore_signal(barrier, inc=1, device_id={"col": partner}, device_id_type=MESH)
    for d in range(1, n_out):
        pl.semaphore_signal(barrier, inc=1, device_id={"col": ahead[d]}, device_id_type=MESH)
    for e in range(1, nr):
        pl.semaphore_signal(barrier, inc=1, device_id={"row": row_at[e]}, device_id_type=MESH)
    pl.semaphore_wait(barrier, n_out + nr - 1)

    started = []

    def go(*args):
        copy = send(*args)
        copy.start()
        started.append(copy)
        return copy

    order = list(range(1, n_out)) + [0]
    pair = {}
    for d in order:
        pair[d] = go(part_ref.at[partner_ahead[d]], from_pair.at[d], p_send.at[d], p_recv.at[d], {"col": partner})
    w_copies = [
        go(wb_ref.at[row_at[e]], w_row.at[e - 1], wr_send.at[e - 1], wr_recv.at[e - 1], {"row": row_at[e]})
        for e in range(1, nr)
    ]
    copies = []
    for d in order:
        pair[d].wait_recv()
        both = part_ref[ahead[d]].astype(F32) + from_pair[d].astype(F32)
        if d:
            send_buf[d - 1] = both.astype(BF16)
            copies.append(go(
                send_buf.at[d - 1], from_chip.at[d - 1], s_send.at[d - 1], s_recv.at[d - 1], {"col": ahead[d]}
            ))
    total = wb_ref[r]
    for e in range(1, nr):
        w_copies[e - 1].wait_recv()
        total = total + w_row[e - 1]
    w_sum[...] = total
    go(w_sum, w_pair, wp_send.at[0], wp_recv.at[0], {"col": partner}).wait_recv()
    w_chip[outer] = w_sum[...] + w_pair[...]
    w_copies = [
        go(w_chip.at[outer], w_chip.at[outer], wc_send.at[d - 1], wc_recv.at[d - 1], {"col": ahead[d]})
        for d in range(1, n_out)
    ]
    for copy in w_copies:
        copy.wait_recv()
    total = w_chip[0]
    for n in range(1, n_out):
        total = total + w_chip[n]
    w_all[r] = total
    w_copies = [
        go(w_all.at[r], w_all.at[r], wa_send.at[e - 1], wa_recv.at[e - 1], {"row": row_at[e]})
        for e in range(1, nr)
    ]
    for copy in copies:
        copy.wait_recv()
    for d in range(1, n_out):
        both = both + from_chip[d - 1].astype(F32)
    out_ref[...] = both.astype(BF16)
    for copy in w_copies:
        copy.wait_recv()
    cut = wg_ref.shape[0] // nr
    for n in range(nr):
        wg_ref[pl.ds(n * cut, cut), :] = w_all[n, pl.ds(0, cut), :]
    bg_ref[...] = w_all[0, pl.ds(cut, 1), :]
    for copy in started:
        copy.wait_send()


def on_device(mesh, features, adjacency, tile_cols, row_counts, weight, bias, out_grad):
    blocks, tile, slot_width = adjacency.shape
    own_rows, feat = features.shape
    nc, nr = mesh.shape["col"], mesh.shape["row"]
    n_out = nc // 2
    col_blocks = nc * own_rows // tile
    scale = 1.0 / math.sqrt(own_rows * nc * nr)
    cut = feat // nr

    vmem = pl.BlockSpec(memory_space=pltpu.VMEM)
    smem = pl.BlockSpec(memory_space=pltpu.SMEM)
    hbm = pl.BlockSpec(memory_space=pltpu.HBM)
    dma = pltpu.SemaphoreType.DMA
    rows = blocks * tile // nr
    tile_flops = 2 * blocks * tile * slot_width * feat
    activations, grads, wb = pl.pallas_call(
        functools.partial(forward_kernel, nc, nr, scale),
        out_shape=(
            jax.ShapeDtypeStruct((rows, feat), BF16),
            jax.ShapeDtypeStruct((blocks * tile, feat), BF16),
            jax.ShapeDtypeStruct((nr, cut + 8, feat), F32),
        ),
        in_specs=[smem, smem, hbm, hbm, hbm, hbm, hbm],
        out_specs=(vmem, vmem, vmem),
        scratch_shapes=[
            pltpu.VMEM((col_blocks + 1, tile, feat), BF16),
            pltpu.VMEM((blocks, tile, slot_width), BF16),
            pltpu.VMEM((feat, feat), BF16),
            pltpu.VMEM((1, feat), F32),
            pltpu.VMEM((rows, feat), BF16),
            pltpu.VMEM((rows, feat), F32),
            pltpu.VMEM((nr - 1, rows, feat), BF16),
            pltpu.VMEM((nr - 1, rows, feat), BF16),
            pltpu.VMEM((nr, rows, feat), BF16),
            dma((4,)), dma((nr,)), dma((n_out,)), dma((n_out,)), dma((n_out,)), dma((n_out,)),
            dma((nr - 1,)), dma((nr - 1,)), dma((nr - 1,)), dma((nr - 1,)),
        ],
        compiler_params=pltpu.CompilerParams(
            collective_id=0, has_side_effects=True, vmem_limit_bytes=60 * MIB
        ),
        cost_estimate=pl.CostEstimate(
            flops=tile_flops, bytes_accessed=adjacency.size * 2, transcendentals=rows * feat
        ),
    )(
        tile_cols, row_counts, features.reshape(own_rows // tile, tile, feat), adjacency, weight,
        bias.reshape(1, -1), out_grad,
    )

    group = math.gcd(blocks, 4)
    partial = pl.pallas_call(
        functools.partial(backward_kernel, group),
        out_shape=jax.ShapeDtypeStruct((col_blocks, tile, feat), BF16),
        in_specs=[smem, smem, hbm, vmem],
        out_specs=vmem,
        scratch_shapes=[
            pltpu.VMEM((blocks, tile, slot_width), BF16),
            dma((blocks // group,)),
        ] + [pltpu.VMEM((col_blocks + 1, tile, feat), F32) for unused in range(2)],
        compiler_params=pltpu.CompilerParams(vmem_limit_bytes=60 * MIB),
        cost_estimate=pl.CostEstimate(
            flops=tile_flops * 8, bytes_accessed=adjacency.size * 2, transcendentals=0
        ),
    )(tile_cols, row_counts, adjacency, grads)

    feature_grad, weight_grad, bias_grad = pl.pallas_call(
        functools.partial(scatter_kernel, nc, nr),
        out_shape=(
            jax.ShapeDtypeStruct((own_rows, feat), BF16),
            jax.ShapeDtypeStruct((feat, feat), F32),
            jax.ShapeDtypeStruct((1, feat), F32),
        ),
        in_specs=[vmem, vmem],
        out_specs=(vmem, vmem, vmem),
        scratch_shapes=[
            pltpu.VMEM((n_out, own_rows, feat), BF16),
            pltpu.VMEM((n_out - 1, own_rows, feat), BF16),
            pltpu.VMEM((n_out - 1, own_rows, feat), BF16),
            pltpu.VMEM((nr - 1, cut + 8, feat), F32),
            pltpu.VMEM((cut + 8, feat), F32),
            pltpu.VMEM((cut + 8, feat), F32),
            pltpu.VMEM((n_out, cut + 8, feat), F32),
            pltpu.VMEM((nr, cut + 8, feat), F32),
            dma((n_out,)), dma((n_out,)), dma((n_out - 1,)), dma((n_out - 1,)),
            dma((nr - 1,)), dma((nr - 1,)), dma((1,)), dma((1,)),
            dma((n_out - 1,)), dma((n_out - 1,)), dma((nr - 1,)), dma((nr - 1,)),
        ],
        compiler_params=pltpu.CompilerParams(
            collective_id=1, has_side_effects=True, vmem_limit_bytes=20 * MIB
        ),
        cost_estimate=pl.CostEstimate(
            flops=own_rows * nc * feat, bytes_accessed=8 * own_rows * nc * feat, transcendentals=0
        ),
    )(partial.reshape(nc, own_rows, feat), wb)
    return (activations, feature_grad, weight_grad, bias_grad.reshape(-1))


def solution(mesh):
    placed = (
        P(("groups", "row", "col"), None),
        P(("groups", "col"), None, "row"),
        P(("groups", "col"), "row"),
        P(("groups", "col"), "row"),
        P(),
        P(),
        P(("groups", "col", "row"), None),
    )
    return jax.shard_map(
        functools.partial(on_device, mesh),
        mesh=mesh,
        in_specs=placed,
        out_specs=(
            P(("groups", "col", "row"), None),
            P(("groups", "row", "col"), None),
            P("groups", None),
            P("groups"),
        ),
        check_vma=False,
    )
```

time: 189 us -> 82.2 us (0.43)
  waiting for transfers between devices: 97.2 us -> 0 us
  between operations: 14.1 us -> 0.7 us
  Pallas kernels: 63.1 us -> 74.7 us
  local copies, waits for them, and re-layouts: 12.6 us -> 6.41 us
    psum x1 -> x0, waiting for transfers between devices: 97.2 us -> none  [on_device(): wb = lax.psum(wb, ('col', 'row'))]
    pallas_call x2, Pallas kernels: 22.6 us -> 34.4 us  [the longest x1 20.4 us: on_device(): pl.pallas_call(functools.partial(scatter_kernel, nc, nr), out_shape=(jax....]
    unnamed x14 -> x12, local copies, waits for them, and re-layouts: 9.79 us -> 6.41 us
  transfers between devices with their start and end apart: 1 -> 0, of which waited for: 1 -> 0; matrix products, arithmetic and copies ran while one was open for 0% -> 0% of each run, Pallas kernels for 12% -> 0%
where the time goes in v1:
time: 82.2 us; the launch traced here: 81.8 us
  Pallas kernels  74.7 us (91%)
  local copies, waits for them, and re-layouts  6.41 us (8%)
    pallas_call x1, Pallas kernels, on_device(): pl.pallas_call(functools.partial(forward_kernel, nc, nr, scale), out_shap...  40.3 us
    pallas_call x1, Pallas kernels, on_device(): pl.pallas_call(functools.partial(scatter_kernel, nc, nr), out_shape=(jax....  20.4 us
    pallas_call x1, Pallas kernels, on_device(): pl.pallas_call(functools.partial(backward_kernel, group), out_shape=jax.S...  14 us
    unnamed x12, local copies, waits for them, and re-layouts  6.41 us

profile of v1, /device:TPU:0, one launch (start us, length us, event | category | flops | bytes accessed | tf_op | source)
XLA Modules:
  0.0 81.8 jit_solution(9715548854101959708)
XLA Ops:
  0.6 1.4 %copy.11.cols_ref = s32[32,22]{1,0:T(8,128)} copy(s32[32,22]{0,1:T(8,128)} %param.9) | data formatting | bytes 5632 | tf_op args[2]
  2.0 1.3 %copy.12.counts_ref = s32[32,1]{1,0:T(8,128)} copy(s32[32,1]{0,1:T(1,128)} %param.10) | data formatting | bytes 256 | tf_op args[3]
  3.4 40.3 %shard_map.102 = (bf16[512,128]{1,0:T(8,128)(2,1)}, bf16[2048,128]{1,0:T(8,128)(2,1)}, f32[4,40,128]{2,1,0:T(8,128)}) custom-call(s32[32,22]{1,0:T(8,128)} %copy.11.cols_ref, s32[32,1]{1,0:T(8,128)} %copy.12.counts_ref, bf16[8,64,128]{2,1,0:T(8,128)(2,1)} %bitcast.6, bf16[32,64,1408]{2,1,0:T(8,128)(2,1)} %adj_hbm.3, bf16[128,128]{1,0:T(8,128)(2,1)} %weight_hbm.1, ...), custom_call_target="tpu_custom_call" | custom-call | flops 738197504 | bytes 5767168 | tf_op jit(solution)/shard_map/pallas_call | solution.py:296
  43.7 0.0 copy-start.1
  43.7 0.0 copy-start.2
  43.7 14.0 %shard_map.103 = bf16[64,64,128]{2,1,0:T(8,128)(2,1)} custom-call(s32[32,22]{1,0:T(8,128)} %copy.11.cols_ref, s32[32,1]{1,0:T(8,128)} %copy.12.counts_ref, bf16[32,64,1408]{2,1,0:T(8,128)(2,1)} %adj_hbm.3, bf16[2048,128]{1,0:T(8,128)(2,1)} %get-tuple-element.11.grad_ref), custom_call_target="tpu_custom_call" | custom-call | flops 5905580032 | bytes 5767168 | tf_op jit(solution)/shard_map/pallas_call | solution.py:330
  57.7 0.0 copy-done.1
  57.7 0.0 copy-start
  57.7 1.2 %copy-done = bf16[64,64,128]{2,1,0:T(8,128)(2,1)S(1)} copy-done((bf16[64,64,128]{2,1,0:T(8,128)(2,1)S(1)}, bf16[64,64,128]{2,1,0:T(8,128)(2,1)}, u32[]{:S(2)}) %copy-start) | copy-done | bytes 1048600
  58.9 20.4 %shard_map.104 = (bf16[512,128]{1,0:T(8,128)(2,1)S(1)}, f32[128,128]{1,0:T(8,128)S(1)}, f32[1,128]{1,0:T(1,128)S(1)}) custom-call(bf16[8,512,128]{2,1,0:T(8,128)(2,1)S(1)} %bitcast.4, f32[4,40,128]{2,1,0:T(8,128)S(1)} %copy-done.1), custom_call_target="tpu_custom_call" | custom-call | flops 524288 | bytes 4194304 | tf_op jit(solution)/shard_map/pallas_call | solution.py:345
  79.3 0.0 copy-done.2
  79.3 0.7 copy.19
  80.0 0.7 copy.20
  80.7 0.6 copy.21
  81.3 0.5 copy.22
Async XLA Ops:
  43.7 14.0 %copy-start.1 = (f32[4,40,128]{2,1,0:T(8,128)S(1)}, f32[4,40,128]{2,1,0:T(8,128)}, u32[]{:S(2)}) copy-start(f32[4,40,128]{2,1,0:T(8,128)} %get-tuple-element.12.wb_ref) | copy-start | bytes 245764
  43.7 35.6 %copy-start.2 = (bf16[512,128]{1,0:T(8,128)(2,1)S(1)}, bf16[512,128]{1,0:T(8,128)(2,1)}, u32[]{:S(2)}) copy-start(bf16[512,128]{1,0:T(8,128)(2,1)} %get-tuple-element.20) | copy-start | bytes 393220
  57.7 1.2 %copy-start = (bf16[64,64,128]{2,1,0:T(8,128)(2,1)S(1)}, bf16[64,64,128]{2,1,0:T(8,128)(2,1)}, u32[]{:S(2)}) copy-start(bf16[64,64,128]{2,1,0:T(8,128)(2,1)} %shard_map.103) | copy-start | bytes 3145732

commit v2 on v1

v2 whole, which is shorter than its diff:
```python
import functools
import math

import jax
import jax.numpy as jnp
from jax import lax
from jax.experimental import pallas as pl
from jax.experimental.pallas import tpu as pltpu
from jax.sharding import PartitionSpec as P

MESH = pl.DeviceIdType.MESH
F32, BF16 = jnp.float32, jnp.bfloat16
MIB = 1024 * 1024


def col_peers(nc):
    c = lax.axis_index("col")
    outer, core, n_out = c // 2, c % 2, nc // 2
    partner = outer * 2 + (1 - core)
    ahead = [lax.rem(outer + d, n_out) * 2 + core for d in range(n_out)]
    behind = [lax.rem(outer - d + n_out, n_out) * 2 + core for d in range(n_out)]
    return c, partner, ahead, behind


def send(src, dst, send_sem, recv_sem, where):
    return pltpu.make_async_remote_copy(
        src_ref=src, dst_ref=dst, send_sem=send_sem, recv_sem=recv_sem,
        device_id=where, device_id_type=MESH,
    )


def enter(nc, nr):
    c, r = lax.axis_index("col"), lax.axis_index("row")
    barrier = pltpu.get_barrier_semaphore()
    for d in range(1, nc):
        pl.semaphore_signal(barrier, inc=1, device_id={"col": lax.rem(c + d, nc)}, device_id_type=MESH)
    for e in range(1, nr):
        pl.semaphore_signal(barrier, inc=1, device_id={"row": lax.rem(r + e, nr)}, device_id_type=MESH)
    pl.semaphore_wait(barrier, nc - 1 + nr - 1)


def forward_kernel(
    nc, nr, scale, cols_ref, counts_ref, feat_hbm, adj_hbm, weight_hbm, bias_hbm, og_hbm,
    act_ref, grads_ref, wb_ref,
    xg, adj, weight_ref, bias_ref, og_ref, own, part, rbuf, gg, w_out, w_in,
    in_sem, a_sem, f_send, f_recv, p_send, p_recv, r_send, r_recv, g_send, g_recv, w_send, w_recv,
):
    blocks, tile, slot_width = adj.shape
    per_row = slot_width // tile
    chunk = blocks // nr
    rows = chunk * tile
    n_out = nc // 2
    own_blocks = feat_hbm.shape[0]
    c, partner, ahead, behind = col_peers(nc)
    r = lax.axis_index("row")
    row_at = [lax.rem(r + e, nr) for e in range(nr)]

    mine = xg.at[pl.ds(c * own_blocks, own_blocks)]
    first = pltpu.make_async_copy(feat_hbm, mine, in_sem.at[0])
    first.start()
    loads = []
    for e in range(nr):
        t = row_at[(e + 1) % nr]
        cut = pl.ds(t * chunk, chunk)
        load = pltpu.make_async_copy(adj_hbm.at[cut], adj.at[cut], a_sem.at[e])
        load.start()
        loads.append(load)
    small = []
    for n, (src, dst) in enumerate(((weight_hbm, weight_ref), (bias_hbm, bias_ref), (og_hbm, og_ref))):
        load = pltpu.make_async_copy(src, dst, in_sem.at[n + 1])
        load.start()
        small.append(load)

    def blocks_of(col):
        return xg.at[pl.ds(col * own_blocks, own_blocks)]

    xg[nc * own_blocks] = jnp.zeros(xg.shape[1:], xg.dtype)
    first.wait()
    enter(nc, nr)

    copies = []
    for d in range(1, n_out):
        copy = send(blocks_of(c), blocks_of(c), f_send.at[d], f_recv.at[d], {"col": ahead[d]})
        copy.start()
        copies.append(copy)
    pair = []
    copy = send(blocks_of(c), blocks_of(c), p_send.at[0], p_recv.at[0], {"col": partner})
    copy.start()
    pair.append(copy)
    for d in range(1, n_out):
        copies[d - 1].wait_recv()
        came = blocks_of(behind[d])
        copy = send(came, came, p_send.at[d], p_recv.at[d], {"col": partner})
        copy.start()
        pair.append(copy)
    for copy in pair:
        copy.wait_recv()
    for copy in copies + pair:
        copy.wait_send()

    pace = math.gcd(chunk, 2)
    row_copies = []
    for e in range(nr):
        far = (e + 1) % nr
        t = row_at[far]
        loads[e].wait()

        def block_rows(n, carry, t=t, far=far):
            for i in range(pace):
                i = n * pace + i
                b = t * chunk + i
                count = counts_ref[0, b]
                picked = [
                    xg[jnp.where(s < count, cols_ref[s, b], nc * own_blocks)] for s in range(per_row)
                ]
                got = jnp.dot(adj[b], jnp.concatenate(picked, axis=0), preferred_element_type=F32)
                cut = pl.ds(pl.multiple_of(i * tile, tile), tile)
                if far:
                    part[far - 1, cut, :] = got.astype(BF16)
                else:
                    own[cut, :] = got
            return carry

        lax.fori_loop(0, chunk // pace, block_rows, 0)
        if far:
            copy = send(
                part.at[far - 1], rbuf.at[far - 1], r_send.at[far - 1], r_recv.at[far - 1], {"row": t}
            )
            copy.start()
            row_copies.append(copy)
    summed = own[...]
    for copy in row_copies:
        copy.wait_recv()
    for e in range(nr - 1):
        summed = summed + rbuf[e].astype(F32)
    hidden = summed.astype(BF16)
    for load in small:
        load.wait()
    preact = jnp.dot(hidden, weight_ref[...], preferred_element_type=F32) + bias_ref[...]
    sig = jax.nn.sigmoid(preact)
    pre_grad = og_ref[...].astype(F32) * (sig * (1.0 + preact * (1.0 - sig)))
    half = pre_grad.astype(BF16)
    dest = lax.dot_general(
        half, weight_ref[...], (((1,), (1,)), ((), ())), preferred_element_type=F32
    )
    gg[r] = dest.astype(BF16)
    grad_copies = []
    for e in range(1, nr):
        copy = send(gg.at[r], gg.at[r], g_send.at[e - 1], g_recv.at[e - 1], {"row": row_at[e]})
        copy.start()
        grad_copies.append(copy)
    act_ref[...] = (preact * sig).astype(BF16)
    feat = hidden.shape[1]
    cut = feat // nc
    w_out[:, pl.ds(0, cut), :] = scale * lax.dot_general(
        hidden, half, (((0,), (0,)), ((), ())), preferred_element_type=F32
    ).reshape(nc, cut, feat)
    w_out[:, pl.ds(cut, 8), :] = jnp.broadcast_to(
        scale * jnp.sum(pre_grad, axis=0, keepdims=True), (nc, 8, feat)
    )
    w_copies = []
    for d in range(1, nc):
        there = lax.rem(c + d, nc)
        copy = send(w_out.at[there], w_in.at[d - 1], w_send.at[d - 1], w_recv.at[d - 1], {"col": there})
        copy.start()
        w_copies.append(copy)
    total = w_out[c]
    for d in range(1, nc):
        w_copies[d - 1].wait_recv()
        total = total + w_in[d - 1]
    wb_ref[...] = total
    for copy in grad_copies:
        copy.wait_recv()
    grads_ref[...] = gg[...].reshape(grads_ref.shape)
    for copy in row_copies + grad_copies + w_copies:
        copy.wait_send()


def backward_kernel(cols_ref, counts_ref, adj_ref, grad_ref, out_ref, *accs):
    blocks, tile, slot_width = adj_ref.shape
    per_row = slot_width // tile
    dead = out_ref.shape[0]
    for acc in accs:
        acc[...] = jnp.zeros_like(acc)

    def block_row(b, carry):
        contrib = lax.dot_general(
            adj_ref[b], grad_ref[pl.ds(pl.multiple_of(b * tile, tile), tile), :],
            (((0,), (0,)), ((), ())), preferred_element_type=F32,
        )
        count = counts_ref[0, b]
        for s in range(per_row):
            acc = accs[s % len(accs)]
            j = jnp.where(s < count, cols_ref[s, b], dead)
            acc[j] = acc[j] + contrib[s * tile : (s + 1) * tile]
        return carry

    lax.fori_loop(0, blocks, block_row, 0)
    total = accs[0][pl.ds(0, dead)]
    for acc in accs[1:]:
        total = total + acc[pl.ds(0, dead)]
    out_ref[...] = total.astype(BF16)


def scatter_kernel(
    nc, nr, part_ref, wb_ref, out_ref, wg_ref, bg_ref,
    from_pair, send_buf, from_chip, w_row, w_all,
    p_send, p_recv, s_send, s_recv, wr_send, wr_recv, wa_send, wa_recv,
):
    n_out = nc // 2
    c, partner, ahead, behind = col_peers(nc)
    r = lax.axis_index("row")
    row_at = [lax.rem(r + e, nr) for e in range(nr)]
    partner_ahead = [x + partner - c for x in ahead]
    enter(nc, nr)

    started = []

    def go(*args):
        copy = send(*args)
        copy.start()
        started.append(copy)
        return copy

    order = list(range(1, n_out)) + [0]
    pair = {}
    for d in order:
        pair[d] = go(part_ref.at[partner_ahead[d]], from_pair.at[d], p_send.at[d], p_recv.at[d], {"col": partner})
    w_row[r] = wb_ref[...]
    w_copies = [
        go(w_row.at[r], w_row.at[r], wr_send.at[e - 1], wr_recv.at[e - 1], {"row": row_at[e]})
        for e in range(1, nr)
    ]
    copies = []
    for d in order:
        pair[d].wait_recv()
        both = part_ref[ahead[d]].astype(F32) + from_pair[d].astype(F32)
        if d:
            send_buf[d - 1] = both.astype(BF16)
            copies.append(go(
                send_buf.at[d - 1], from_chip.at[d - 1], s_send.at[d - 1], s_recv.at[d - 1], {"col": ahead[d]}
            ))
    for copy in w_copies:
        copy.wait_recv()
    total = w_row[0]
    for n in range(1, nr):
        total = total + w_row[n]
    w_all[c] = total
    w_copies = []
    for d in range(1, nc):
        where = {"col": lax.rem(c + d, nc)}
        w_copies.append(go(w_all.at[c], w_all.at[c], wa_send.at[d - 1], wa_recv.at[d - 1], where))
    for copy in copies:
        copy.wait_recv()
    for d in range(1, n_out):
        both = both + from_chip[d - 1].astype(F32)
    out_ref[...] = both.astype(BF16)
    for copy in w_copies:
        copy.wait_recv()
    cut = wg_ref.shape[0] // nc
    for n in range(nc):
        wg_ref[pl.ds(n * cut, cut), :] = w_all[n, pl.ds(0, cut), :]
    bg_ref[...] = w_all[0, pl.ds(cut, 1), :]
    for copy in started:
        copy.wait_send()


def on_device(mesh, features, adjacency, tile_cols, row_counts, weight, bias, out_grad):
    blocks, tile, slot_width = adjacency.shape
    own_rows, feat = features.shape
    nc, nr = mesh.shape["col"], mesh.shape["row"]
    n_out = nc // 2
    col_blocks = nc * own_rows // tile
    scale = 1.0 / math.sqrt(own_rows * nc * nr)
    cut = feat // nc

    vmem = pl.BlockSpec(memory_space=pltpu.VMEM)
    smem = pl.BlockSpec(memory_space=pltpu.SMEM)
    hbm = pl.BlockSpec(memory_space=pltpu.HBM)
    dma = pltpu.SemaphoreType.DMA
    rows = blocks * tile // nr
    tile_flops = 2 * blocks * tile * slot_width * feat
    activations, grads, wb = pl.pallas_call(
        functools.partial(forward_kernel, nc, nr, scale),
        out_shape=(
            jax.ShapeDtypeStruct((rows, feat), BF16),
            jax.ShapeDtypeStruct((blocks * tile, feat), BF16),
            jax.ShapeDtypeStruct((cut + 8, feat), F32),
        ),
        in_specs=[smem, smem, hbm, hbm, hbm, hbm, hbm],
        out_specs=(vmem, vmem, vmem),
        scratch_shapes=[
            pltpu.VMEM((col_blocks + 1, tile, feat), BF16),
            pltpu.VMEM(adjacency.shape, BF16),
            pltpu.VMEM((feat, feat), BF16),
            pltpu.VMEM((1, feat), F32),
            pltpu.VMEM((rows, feat), BF16),
            pltpu.VMEM((rows, feat), F32),
            pltpu.VMEM((nr - 1, rows, feat), BF16),
            pltpu.VMEM((nr - 1, rows, feat), BF16),
            pltpu.VMEM((nr, rows, feat), BF16),
            pltpu.VMEM((nc, cut + 8, feat), F32),
            pltpu.VMEM((nc - 1, cut + 8, feat), F32),
            dma((4,)), dma((nr,)), dma((n_out,)), dma((n_out,)), dma((n_out,)), dma((n_out,)),
            dma((nr - 1,)), dma((nr - 1,)), dma((nr - 1,)), dma((nr - 1,)), dma((nc - 1,)), dma((nc - 1,)),
        ],
        compiler_params=pltpu.CompilerParams(
            collective_id=0, has_side_effects=True, vmem_limit_bytes=56 * MIB
        ),
        cost_estimate=pl.CostEstimate(
            flops=tile_flops, bytes_accessed=adjacency.size * 2, transcendentals=rows * feat
        ),
    )(
        tile_cols.T, row_counts.T, features.reshape(own_rows // tile, tile, feat), adjacency, weight,
        bias.reshape(1, -1), out_grad,
    )

    partial = pl.pallas_call(
        backward_kernel,
        out_shape=jax.ShapeDtypeStruct((col_blocks, tile, feat), BF16),
        in_specs=[smem, smem, vmem, vmem],
        out_specs=vmem,
        scratch_shapes=[pltpu.VMEM((col_blocks + 1, tile, feat), F32) for unused in range(2)],
        compiler_params=pltpu.CompilerParams(vmem_limit_bytes=32 * MIB),
        cost_estimate=pl.CostEstimate(
            flops=tile_flops * 8, bytes_accessed=adjacency.size * 2, transcendentals=0
        ),
    )(tile_cols.T, row_counts.T, adjacency, grads)

    feature_grad, weight_grad, bias_grad = pl.pallas_call(
        functools.partial(scatter_kernel, nc, nr),
        out_shape=(
            jax.ShapeDtypeStruct((own_rows, feat), BF16),
            jax.ShapeDtypeStruct((feat, feat), F32),
            jax.ShapeDtypeStruct((1, feat), F32),
        ),
        in_specs=[vmem, vmem],
        out_specs=(vmem, vmem, vmem),
        scratch_shapes=[
            pltpu.VMEM((n_out, own_rows, feat), BF16),
            pltpu.VMEM((n_out - 1, own_rows, feat), BF16),
            pltpu.VMEM((n_out - 1, own_rows, feat), BF16),
            pltpu.VMEM((nr, cut + 8, feat), F32),
            pltpu.VMEM((nc, cut + 8, feat), F32),
            dma((n_out,)), dma((n_out,)), dma((n_out - 1,)), dma((n_out - 1,)),
            dma((nr - 1,)), dma((nr - 1,)), dma((nc - 1,)), dma((nc - 1,)),
        ],
        compiler_params=pltpu.CompilerParams(
            collective_id=1, has_side_effects=True, vmem_limit_bytes=20 * MIB
        ),
        cost_estimate=pl.CostEstimate(
            flops=own_rows * nc * feat, bytes_accessed=8 * own_rows * nc * feat, transcendentals=0
        ),
    )(partial.reshape(nc, own_rows, feat), wb)
    return (activations, feature_grad, weight_grad, bias_grad.reshape(-1))


def solution(mesh):
    placed = (
        P(("groups", "row", "col"), None),
        P(("groups", "col"), None, "row"),
        P(("groups", "col"), "row"),
        P(("groups", "col"), "row"),
        P(),
        P(),
        P(("groups", "col", "row"), None),
    )
    return jax.shard_map(
        functools.partial(on_device, mesh),
        mesh=mesh,
        in_specs=placed,
        out_specs=(
            P(("groups", "col", "row"), None),
            P(("groups", "row", "col"), None),
            P("groups", None),
            P("groups"),
        ),
        check_vma=False,
    )
```

time: 82.2 us -> 75.3 us (0.916)
  Pallas kernels: 74.7 us -> 70.9 us
  local copies, waits for them, and re-layouts: 6.41 us -> 3.51 us
    unnamed x12 -> x16, local copies, waits for them, and re-layouts: 6.41 us -> 3.51 us
    pallas_call x1, Pallas kernels: 20.4 us -> 17.9 us  [on_device(): pl.pallas_call(functools.partial(scatter_kernel, nc, nr), out_shape=(jax....]
    pallas_call x1, Pallas kernels: 14 us -> 11.5 us  [on_device(): pl.pallas_call(backward_kernel, out_shape=jax.ShapeDtypeStruct((col_block...]
    pallas_call x1, Pallas kernels: 40.3 us -> 41.5 us  [on_device(): pl.pallas_call(functools.partial(forward_kernel, nc, nr, scale), out_shap...]
where the time goes in v2:
time: 75.3 us; the launch traced here: 75.1 us
  Pallas kernels  70.9 us (94%)
  local copies, waits for them, and re-layouts  3.51 us (5%)
    pallas_call x1, Pallas kernels, on_device(): pl.pallas_call(functools.partial(forward_kernel, nc, nr, scale), out_shap...  41.5 us
    pallas_call x1, Pallas kernels, on_device(): pl.pallas_call(functools.partial(scatter_kernel, nc, nr), out_shape=(jax....  17.9 us
    pallas_call x1, Pallas kernels, on_device(): pl.pallas_call(backward_kernel, out_shape=jax.ShapeDtypeStruct((col_block...  11.5 us
    unnamed x16, local copies, waits for them, and re-layouts  3.51 us

profile of v2, /device:TPU:0, one launch (start us, length us, event | category | flops | bytes accessed | tf_op | source)
XLA Modules:
  0.0 75.1 jit_solution(9968338214998417372)
XLA Ops:
  0.6 0.0 copy-start
  0.6 0.0 copy-start.3
  0.7 0.0 copy-start.2
  0.7 41.5 %shard_map.102 = (bf16[512,128]{1,0:T(8,128)(2,1)}, bf16[2048,128]{1,0:T(8,128)(2,1)}, f32[24,128]{1,0:T(8,128)}) custom-call(s32[22,32]{1,0:T(8,128)} %bitcast.7, s32[1,32]{1,0:T(1,128)} %bitcast.9, bf16[8,64,128]{2,1,0:T(8,128)(2,1)} %bitcast.12, bf16[32,64,1408]{2,1,0:T(8,128)(2,1)} %adj_ref.1, bf16[128,128]{1,0:T(8,128)(2,1)} %weight_hbm.1, ...), custom_call_target="tpu_custom_call" | custom-call | flops 738197504 | bytes 5767168 | tf_op jit(solution)/shard_map/pallas_call | solution.py:283
  42.2 0.0 copy-done
  42.2 0.0 copy-done.3
  42.2 0.0 copy-done.2
  42.2 0.0 copy-start.4
  42.3 1.0 %copy-done.4 = bf16[2048,128]{1,0:T(8,128)(2,1)S(1)} copy-done((bf16[2048,128]{1,0:T(8,128)(2,1)S(1)}, bf16[2048,128]{1,0:T(8,128)(2,1)}, u32[]{:S(2)}) %copy-start.4) | copy-done | bytes 524312
  43.3 0.0 copy-start.1
  43.3 0.0 copy-start.5
  43.3 11.5 %shard_map.103 = bf16[64,64,128]{2,1,0:T(8,128)(2,1)S(1)} custom-call(s32[22,32]{1,0:T(8,128)S(1)} %bitcast.8, s32[1,32]{1,0:T(1,128)S(1)} %bitcast.10, bf16[32,64,1408]{2,1,0:T(8,128)(2,1)S(1)} %copy-done, bf16[2048,128]{1,0:T(8,128)(2,1)S(1)} %copy-done.4), custom_call_target="tpu_custom_call" | custom-call | flops 5905580032 | bytes 5767168 | tf_op jit(solution)/shard_map/pallas_call | solution.py:318
  54.8 0.0 copy-done.1
  54.8 17.9 %shard_map.104 = (bf16[512,128]{1,0:T(8,128)(2,1)S(1)}, f32[128,128]{1,0:T(8,128)S(1)}, f32[1,128]{1,0:T(1,128)S(1)}) custom-call(bf16[8,512,128]{2,1,0:T(8,128)(2,1)S(1)} %bitcast.6, f32[24,128]{1,0:T(8,128)S(1)} %copy-done.1), custom_call_target="tpu_custom_call" | custom-call | flops 524288 | bytes 4194304 | tf_op jit(solution)/shard_map/pallas_call | solution.py:330
  72.7 0.0 copy-done.5
  72.7 0.7 copy.15
  73.3 0.7 copy.16
  74.0 0.6 copy.17
  74.6 0.5 copy.18
Async XLA Ops:
  0.6 41.6 %copy-start = (bf16[32,64,1408]{2,1,0:T(8,128)(2,1)S(1)}, bf16[32,64,1408]{2,1,0:T(8,128)(2,1)}, u32[]{:S(2)}) copy-start(bf16[32,64,1408]{2,1,0:T(8,128)(2,1)} %adj_ref.1) | copy-start | bytes 17301508
  0.6 41.6 %copy-start.3 = (s32[32,1]{0,1:T(1,128)S(1)}, s32[32,1]{0,1:T(1,128)}, u32[]{:S(2)}) copy-start(s32[32,1]{0,1:T(1,128)} %param.10) | copy-start | bytes 388
  0.7 41.6 %copy-start.2 = (s32[32,22]{0,1:T(8,128)S(1)}, s32[32,22]{0,1:T(8,128)}, u32[]{:S(2)}) copy-start(s32[32,22]{0,1:T(8,128)} %param.9) | copy-start | bytes 8452
  42.2 1.0 %copy-start.4 = (bf16[2048,128]{1,0:T(8,128)(2,1)S(1)}, bf16[2048,128]{1,0:T(8,128)(2,1)}, u32[]{:S(2)}) copy-start(bf16[2048,128]{1,0:T(8,128)(2,1)} %get-tuple-element.11.grad_ref) | copy-start | bytes 1572868
  43.3 11.5 %copy-start.1 = (f32[24,128]{1,0:T(8,128)S(1)}, f32[24,128]{1,0:T(8,128)}, u32[]{:S(2)}) copy-start(f32[24,128]{1,0:T(8,128)} %get-tuple-element.12.wb_ref) | copy-start | bytes 36868
  43.3 29.4 %copy-start.5 = (bf16[512,128]{1,0:T(8,128)(2,1)S(1)}, bf16[512,128]{1,0:T(8,128)(2,1)}, u32[]{:S(2)}) copy-start(bf16[512,128]{1,0:T(8,128)(2,1)} %get-tuple-element.20) | copy-start | bytes 393220

commit v3 on v2

--- a/solution.py
+++ b/solution.py
@@ -42,8 +42,8 @@
 def forward_kernel(
     nc, nr, scale, cols_ref, counts_ref, feat_hbm, adj_hbm, weight_hbm, bias_hbm, og_hbm,
     act_ref, grads_ref, wb_ref,
-    xg, adj, weight_ref, bias_ref, og_ref, own, part, rbuf, gg, w_out, w_in,
-    in_sem, a_sem, f_send, f_recv, p_send, p_recv, r_send, r_recv, g_send, g_recv, w_send, w_recv,
+    xg, adj, weight_ref, bias_ref, og_ref, own, part, rbuf, gg, w_out, w_in, w_all,
+    in_sem, a_sem, f_send, f_recv, p_send, p_recv, r_send, r_recv, g_send, g_recv, w_send, w_recv, wa_send, wa_recv,
 ):
     blocks, tile, slot_width = adj.shape
     per_row = slot_width // tile
@@ -144,11 +144,15 @@
         half, weight_ref[...], (((1,), (1,)), ((), ())), preferred_element_type=F32
     )
     gg[r] = dest.astype(BF16)
-    grad_copies = []
-    for e in range(1, nr):
-        copy = send(gg.at[r], gg.at[r], g_send.at[e - 1], g_recv.at[e - 1], {"row": row_at[e]})
-        copy.start()
-        grad_copies.append(copy)
+
+    def hop(t, step):
+        way = 0 if step > 0 else 1
+        return send(gg.at[t], gg.at[t], g_send.at[way, t], g_recv.at[t], {"row": r + step})
+
+    for step in (1, -1):
+        @pl.when((r + step >= 0) & (r + step < nr))
+        def start_chain(step=step):
+            hop(r, step).start()
     act_ref[...] = (preact * sig).astype(BF16)
     feat = hidden.shape[1]
     cut = feat // nc
@@ -164,15 +168,43 @@
         copy = send(w_out.at[there], w_in.at[d - 1], w_send.at[d - 1], w_recv.at[d - 1], {"col": there})
         copy.start()
         w_copies.append(copy)
-    total = w_out[c]
-    for d in range(1, nc):
-        w_copies[d - 1].wait_recv()
-        total = total + w_in[d - 1]
-    wb_ref[...] = total
-    for copy in grad_copies:
+    for k in range(1, nr):
+        if k == min(2, nr - 1):
+            total = w_out[c]
+            for d in range(1, nc):
+                w_copies[d - 1].wait_recv()
+                total = total + w_in[d - 1]
+            w_all[c] = total
+            for d in range(1, nc):
+                there = lax.rem(c + d, nc)
+                copy = send(w_all.at[c], w_all.at[c], wa_send.at[d - 1], wa_recv.at[d - 1], {"col": there})
+                copy.start()
+                w_copies.append(copy)
+        for step in (1, -1):
+            t = r - k * step
+            came = (t >= 0) & (t < nr)
+
+            @pl.when(came)
+            def arrive(t=t, step=step):
+                hop(t, step).wait_recv()
+
+            @pl.when(came & (r + step >= 0) & (r + step < nr))
+            def pass_on(t=t, step=step):
+                hop(t, step).start()
+    for k in range(nr):
+        for step in (1, -1):
+            t = r - k * step
+
+            @pl.when((t >= 0) & (t < nr) & (r + step >= 0) & (r + step < nr))
+            def sent(t=t, step=step):
+                hop(t, step).wait_send()
+    for copy in w_copies[nc - 1 :]:
         copy.wait_recv()
+    for n in range(nc):
+        wb_ref[pl.ds(n * cut, cut), :] = w_all[n, pl.ds(0, cut), :]
+    wb_ref[pl.ds(feat, 8), :] = w_all[0, pl.ds(cut, 8), :]
     grads_ref[...] = gg[...].reshape(grads_ref.shape)
-    for copy in row_copies + grad_copies + w_copies:
+    for copy in row_copies + w_copies:
         copy.wait_send()
 
 
@@ -183,19 +215,25 @@
     for acc in accs:
         acc[...] = jnp.zeros_like(acc)
 
-    def block_row(b, carry):
-        contrib = lax.dot_general(
-            adj_ref[b], grad_ref[pl.ds(pl.multiple_of(b * tile, tile), tile), :],
-            (((0,), (0,)), ((), ())), preferred_element_type=F32,
-        )
-        count = counts_ref[0, b]
+    pace = math.gcd(blocks, 2)
+
+    def block_rows(n, carry):
+        contribs = []
+        for i in range(pace):
+            b = n * pace + i
+            contribs.append(lax.dot_general(
+                adj_ref[b], grad_ref[pl.ds(pl.multiple_of(b * tile, tile), tile), :],
+                (((0,), (0,)), ((), ())), preferred_element_type=F32,
+            ))
         for s in range(per_row):
-            acc = accs[s % len(accs)]
-            j = jnp.where(s < count, cols_ref[s, b], dead)
-            acc[j] = acc[j] + contrib[s * tile : (s + 1) * tile]
+            for i in range(pace):
+                b = n * pace + i
+                acc = accs[2 * i + s % 2]
+                j = jnp.where(s < counts_ref[0, b], cols_ref[s, b], dead)
+                acc[j] = acc[j] + contribs[i][s * tile : (s + 1) * tile]
         return carry
 
-    lax.fori_loop(0, blocks, block_row, 0)
+    lax.fori_loop(0, blocks // pace, block_rows, 0)
     total = accs[0][pl.ds(0, dead)]
     for acc in accs[1:]:
         total = total + acc[pl.ds(0, dead)]
@@ -204,8 +242,8 @@
 
 def scatter_kernel(
     nc, nr, part_ref, wb_ref, out_ref, wg_ref, bg_ref,
-    from_pair, send_buf, from_chip, w_row, w_all,
-    p_send, p_recv, s_send, s_recv, wr_send, wr_recv, wa_send, wa_recv,
+    from_pair, send_buf, from_chip, w_row,
+    p_send, p_recv, s_send, s_recv, wr_send, wr_recv,
 ):
     n_out = nc // 2
     c, partner, ahead, behind = col_peers(nc)
@@ -240,16 +278,6 @@
             copies.append(go(
                 send_buf.at[d - 1], from_chip.at[d - 1], s_send.at[d - 1], s_recv.at[d - 1], {"col": ahead[d]}
             ))
-    for copy in w_copies:
-        copy.wait_recv()
-    total = w_row[0]
-    for n in range(1, nr):
-        total = total + w_row[n]
-    w_all[c] = total
-    w_copies = []
-    for d in range(1, nc):
-        where = {"col": lax.rem(c + d, nc)}
-        w_copies.append(go(w_all.at[c], w_all.at[c], wa_send.at[d - 1], wa_recv.at[d - 1], where))
     for copy in copies:
         copy.wait_recv()
     for d in range(1, n_out):
@@ -257,10 +285,12 @@
     out_ref[...] = both.astype(BF16)
     for copy in w_copies:
         copy.wait_recv()
-    cut = wg_ref.shape[0] // nc
-    for n in range(nc):
-        wg_ref[pl.ds(n * cut, cut), :] = w_all[n, pl.ds(0, cut), :]
-    bg_ref[...] = w_all[0, pl.ds(cut, 1), :]
+    total = w_row[0]
+    for n in range(1, nr):
+        total = total + w_row[n]
+    feat = wg_ref.shape[0]
+    wg_ref[...] = total[:feat]
+    bg_ref[...] = total[feat : feat + 1]
     for copy in started:
         copy.wait_send()
 
@@ -285,7 +315,7 @@
         out_shape=(
             jax.ShapeDtypeStruct((rows, feat), BF16),
             jax.ShapeDtypeStruct((blocks * tile, feat), BF16),
-            jax.ShapeDtypeStruct((cut + 8, feat), F32),
+            jax.ShapeDtypeStruct((feat + 8, feat), F32),
         ),
         in_specs=[smem, smem, hbm, hbm, hbm, hbm, hbm],
         out_specs=(vmem, vmem, vmem),
@@ -301,8 +331,10 @@
             pltpu.VMEM((nr, rows, feat), BF16),
             pltpu.VMEM((nc, cut + 8, feat), F32),
             pltpu.VMEM((nc - 1, cut + 8, feat), F32),
+            pltpu.VMEM((nc, cut + 8, feat), F32),
             dma((4,)), dma((nr,)), dma((n_out,)), dma((n_out,)), dma((n_out,)), dma((n_out,)),
-            dma((nr - 1,)), dma((nr - 1,)), dma((nr - 1,)), dma((nr - 1,)), dma((nc - 1,)), dma((nc - 1,)),
+            dma((nr - 1,)), dma((nr - 1,)), dma((2, nr)), dma((nr,)),
+            dma((nc - 1,)), dma((nc - 1,)), dma((nc - 1,)), dma((nc - 1,)),
         ],
         compiler_params=pltpu.CompilerParams(
             collective_id=0, has_side_effects=True, vmem_limit_bytes=56 * MIB
@@ -320,7 +352,7 @@
         out_shape=jax.ShapeDtypeStruct((col_blocks, tile, feat), BF16),
         in_specs=[smem, smem, vmem, vmem],
         out_specs=vmem,
-        scratch_shapes=[pltpu.VMEM((col_blocks + 1, tile, feat), F32) for unused in range(2)],
+        scratch_shapes=[pltpu.VMEM((col_blocks + 1, tile, feat), F32) for unused in range(4)],
         compiler_params=pltpu.CompilerParams(vmem_limit_bytes=32 * MIB),
         cost_estimate=pl.CostEstimate(
             flops=tile_flops * 8, bytes_accessed=adjacency.size * 2, transcendentals=0
@@ -340,10 +372,9 @@
             pltpu.VMEM((n_out, own_rows, feat), BF16),
             pltpu.VMEM((n_out - 1, own_rows, feat), BF16),
             pltpu.VMEM((n_out - 1, own_rows, feat), BF16),
-            pltpu.VMEM((nr, cut + 8, feat), F32),
-            pltpu.VMEM((nc, cut + 8, feat), F32),
+            pltpu.VMEM((nr, feat + 8, feat), F32),
             dma((n_out,)), dma((n_out,)), dma((n_out - 1,)), dma((n_out - 1,)),
-            dma((nr - 1,)), dma((nr - 1,)), dma((nc - 1,)), dma((nc - 1,)),
+            dma((nr - 1,)), dma((nr - 1,)),
         ],
         compiler_params=pltpu.CompilerParams(
             collective_id=1, has_side_effects=True, vmem_limit_bytes=20 * MIB

time: 75.3 us -> 70.1 us (0.931)
  Pallas kernels: 70.9 us -> 65.7 us
    pallas_call x1, Pallas kernels: 17.9 us -> 11.2 us  [on_device(): pl.pallas_call(functools.partial(scatter_kernel, nc, nr), out_shape=(jax....]
    pallas_call x1, Pallas kernels: 41.5 us -> 46.6 us  [on_device(): pl.pallas_call(functools.partial(forward_kernel, nc, nr, scale), out_shap...]
    pallas_call x1, Pallas kernels: 11.5 us -> 7.89 us  [on_device(): pl.pallas_call(backward_kernel, out_shape=jax.ShapeDtypeStruct((col_block...]
where the time goes in v3:
time: 70.1 us; the launch traced here: 69.9 us
  Pallas kernels  65.7 us (94%)
  local copies, waits for them, and re-layouts  3.51 us (5%)
  between operations  0.73 us (1%)
    pallas_call x1, Pallas kernels, on_device(): pl.pallas_call(functools.partial(forward_kernel, nc, nr, scale), out_shap...  46.6 us
    pallas_call x1, Pallas kernels, on_device(): pl.pallas_call(functools.partial(scatter_kernel, nc, nr), out_shape=(jax....  11.2 us
    pallas_call x1, Pallas kernels, on_device(): pl.pallas_call(backward_kernel, out_shape=jax.ShapeDtypeStruct((col_block...  7.89 us
    unnamed x16, local copies, waits for them, and re-layouts  3.51 us

profile of v3, /device:TPU:0, one launch (start us, length us, event | category | flops | bytes accessed | tf_op | source)
XLA Modules:
  0.0 69.9 jit_solution(4266798190273961369)
XLA Ops:
  0.6 0.0 copy-start
  0.6 0.0 copy-start.3
  0.7 0.0 copy-start.2
  0.7 46.6 %shard_map.102 = (bf16[512,128]{1,0:T(8,128)(2,1)}, bf16[2048,128]{1,0:T(8,128)(2,1)}, f32[136,128]{1,0:T(8,128)}) custom-call(s32[22,32]{1,0:T(8,128)} %bitcast.7, s32[1,32]{1,0:T(1,128)} %bitcast.9, bf16[8,64,128]{2,1,0:T(8,128)(2,1)} %bitcast.12, bf16[32,64,1408]{2,1,0:T(8,128)(2,1)} %adj_ref.1, bf16[128,128]{1,0:T(8,128)(2,1)} %weight_hbm.1, ...), custom_call_target="tpu_custom_call" | custom-call | flops 738197504 | bytes 5767168 | tf_op jit(solution)/shard_map/pallas_call | solution.py:313
  47.2 0.0 copy-done
  47.3 0.0 copy-done.3
  47.3 0.0 copy-done.2
  47.3 0.0 copy-start.4
  47.3 1.0 %copy-done.4 = bf16[2048,128]{1,0:T(8,128)(2,1)S(1)} copy-done((bf16[2048,128]{1,0:T(8,128)(2,1)S(1)}, bf16[2048,128]{1,0:T(8,128)(2,1)}, u32[]{:S(2)}) %copy-start.4) | copy-done | bytes 524312
  48.3 0.0 copy-start.1
  48.3 0.0 copy-start.5
  48.3 7.9 %shard_map.103 = bf16[64,64,128]{2,1,0:T(8,128)(2,1)S(1)} custom-call(s32[22,32]{1,0:T(8,128)S(1)} %bitcast.8, s32[1,32]{1,0:T(1,128)S(1)} %bitcast.10, bf16[32,64,1408]{2,1,0:T(8,128)(2,1)S(1)} %copy-done, bf16[2048,128]{1,0:T(8,128)(2,1)S(1)} %copy-done.4), custom_call_target="tpu_custom_call" | custom-call | flops 5905580032 | bytes 5767168 | tf_op jit(solution)/shard_map/pallas_call | solution.py:350
  56.2 0.0 copy-done.1
  56.2 11.2 %shard_map.104 = (bf16[512,128]{1,0:T(8,128)(2,1)S(1)}, f32[128,128]{1,0:T(8,128)S(1)}, f32[1,128]{1,0:T(1,128)S(1)}) custom-call(bf16[8,512,128]{2,1,0:T(8,128)(2,1)S(1)} %bitcast.6, f32[136,128]{1,0:T(8,128)S(1)} %copy-done.1), custom_call_target="tpu_custom_call" | custom-call | flops 524288 | bytes 4194304 | tf_op jit(solution)/shard_map/pallas_call | solution.py:362
  67.5 0.0 copy-done.5
  67.5 0.7 copy.15
  68.1 0.7 copy.16
  68.8 0.6 copy.17
  69.4 0.5 copy.18
Async XLA Ops:
  0.6 46.6 %copy-start = (bf16[32,64,1408]{2,1,0:T(8,128)(2,1)S(1)}, bf16[32,64,1408]{2,1,0:T(8,128)(2,1)}, u32[]{:S(2)}) copy-start(bf16[32,64,1408]{2,1,0:T(8,128)(2,1)} %adj_ref.1) | copy-start | bytes 17301508
  0.6 46.6 %copy-start.3 = (s32[32,1]{0,1:T(1,128)S(1)}, s32[32,1]{0,1:T(1,128)}, u32[]{:S(2)}) copy-start(s32[32,1]{0,1:T(1,128)} %param.10) | copy-start | bytes 388
  0.7 46.6 %copy-start.2 = (s32[32,22]{0,1:T(8,128)S(1)}, s32[32,22]{0,1:T(8,128)}, u32[]{:S(2)}) copy-start(s32[32,22]{0,1:T(8,128)} %param.9) | copy-start | bytes 8452
  47.3 1.0 %copy-start.4 = (bf16[2048,128]{1,0:T(8,128)(2,1)S(1)}, bf16[2048,128]{1,0:T(8,128)(2,1)}, u32[]{:S(2)}) copy-start(bf16[2048,128]{1,0:T(8,128)(2,1)} %get-tuple-element.11.grad_ref) | copy-start | bytes 1572868
  48.3 7.9 %copy-start.1 = (f32[136,128]{1,0:T(8,128)S(1)}, f32[136,128]{1,0:T(8,128)}, u32[]{:S(2)}) copy-start(f32[136,128]{1,0:T(8,128)} %get-tuple-element.12.wb_ref) | copy-start | bytes 208900
  48.3 19.2 %copy-start.5 = (bf16[512,128]{1,0:T(8,128)(2,1)S(1)}, bf16[512,128]{1,0:T(8,128)(2,1)}, u32[]{:S(2)}) copy-start(bf16[512,128]{1,0:T(8,128)(2,1)} %get-tuple-element.20) | copy-start | bytes 393220

commit v4 on v3

--- a/solution.py
+++ b/solution.py
@@ -98,7 +98,7 @@
     for copy in copies + pair:
         copy.wait_send()
 
-    pace = math.gcd(chunk, 2)
+    pace = math.gcd(chunk, 4)
     row_copies = []
     for e in range(nr):
         far = (e + 1) % nr
@@ -208,14 +208,16 @@
         copy.wait_send()
 
 
-def backward_kernel(cols_ref, counts_ref, adj_ref, grad_ref, out_ref, *accs):
+def backward_kernel(cols_ref, counts_ref, adj_ref, grad_ref, act_hbm, out_ref, act_out, sem, *accs):
     blocks, tile, slot_width = adj_ref.shape
     per_row = slot_width // tile
     dead = out_ref.shape[0]
+    hand_out = pltpu.make_async_copy(act_hbm, act_out, sem)
+    hand_out.start()
     for acc in accs:
         acc[...] = jnp.zeros_like(acc)
 
-    pace = math.gcd(blocks, 2)
+    pace = math.gcd(blocks, 4)
 
     def block_rows(n, carry):
         contribs = []
@@ -228,7 +230,7 @@
         for s in range(per_row):
             for i in range(pace):
                 b = n * pace + i
-                acc = accs[2 * i + s % 2]
+                acc = accs[i]
                 j = jnp.where(s < counts_ref[0, b], cols_ref[s, b], dead)
                 acc[j] = acc[j] + contribs[i][s * tile : (s + 1) * tile]
         return carry
@@ -238,6 +240,7 @@
     for acc in accs[1:]:
         total = total + acc[pl.ds(0, dead)]
     out_ref[...] = total.astype(BF16)
+    hand_out.wait()
 
 
 def scatter_kernel(
@@ -347,17 +350,20 @@
         bias.reshape(1, -1), out_grad,
     )
 
-    partial = pl.pallas_call(
+    partial, activations = pl.pallas_call(
         backward_kernel,
-        out_shape=jax.ShapeDtypeStruct((col_blocks, tile, feat), BF16),
-        in_specs=[smem, smem, vmem, vmem],
-        out_specs=vmem,
-        scratch_shapes=[pltpu.VMEM((col_blocks + 1, tile, feat), F32) for unused in range(4)],
+        out_shape=(
+            jax.ShapeDtypeStruct((col_blocks, tile, feat), BF16),
+            jax.ShapeDtypeStruct((rows, feat), BF16),
+        ),
+        in_specs=[smem, smem, vmem, vmem, hbm],
+        out_specs=(vmem, hbm),
+        scratch_shapes=[dma] + [pltpu.VMEM((col_blocks + 1, tile, feat), F32) for unused in range(4)],
         compiler_params=pltpu.CompilerParams(vmem_limit_bytes=32 * MIB),
         cost_estimate=pl.CostEstimate(
             flops=tile_flops * 8, bytes_accessed=adjacency.size * 2, transcendentals=0
         ),
-    )(tile_cols.T, row_counts.T, adjacency, grads)
+    )(tile_cols.T, row_counts.T, adjacency, grads, activations)
 
     feature_grad, weight_grad, bias_grad = pl.pallas_call(
         functools.partial(scatter_kernel, nc, nr),

time: 70.1 us -> 68.8 us (0.981)
  Pallas kernels: 65.7 us -> 64.1 us
    pallas_call x1, Pallas kernels: 7.89 us -> 6.51 us  [on_device(): pl.pallas_call(backward_kernel, out_shape=(jax.ShapeDtypeStruct((col_bloc...]
    unnamed x16 -> x15, local copies, waits for them, and re-layouts: 3.51 us -> 3.75 us
where the time goes in v4:
time: 68.8 us; the launch traced here: 68.6 us
  Pallas kernels  64.1 us (93%)
  local copies, waits for them, and re-layouts  3.75 us (5%)
  between operations  0.72 us (1%)
    pallas_call x1, Pallas kernels, on_device(): pl.pallas_call(functools.partial(forward_kernel, nc, nr, scale), out_shap...  46.4 us
    pallas_call x1, Pallas kernels, on_device(): pl.pallas_call(functools.partial(scatter_kernel, nc, nr), out_shape=(jax....  11.2 us
    pallas_call x1, Pallas kernels, on_device(): pl.pallas_call(backward_kernel, out_shape=(jax.ShapeDtypeStruct((col_bloc...  6.51 us
    unnamed x15, local copies, waits for them, and re-layouts  3.75 us

profile of v4, /device:TPU:0, one launch (start us, length us, event | category | flops | bytes accessed | tf_op | source)
XLA Modules:
  0.0 68.6 jit_solution(945217968431424350)
XLA Ops:
  0.6 0.0 copy-start
  0.6 0.0 copy-start.3
  0.7 0.0 copy-start.2
  0.7 46.4 %shard_map.102 = (bf16[512,128]{1,0:T(8,128)(2,1)}, bf16[2048,128]{1,0:T(8,128)(2,1)}, f32[136,128]{1,0:T(8,128)}) custom-call(s32[22,32]{1,0:T(8,128)} %bitcast.7, s32[1,32]{1,0:T(1,128)} %bitcast.9, bf16[8,64,128]{2,1,0:T(8,128)(2,1)} %bitcast.12, bf16[32,64,1408]{2,1,0:T(8,128)(2,1)} %adj_ref.1, bf16[128,128]{1,0:T(8,128)(2,1)} %weight_hbm.1, ...), custom_call_target="tpu_custom_call" | custom-call | flops 738197504 | bytes 5767168 | tf_op jit(solution)/shard_map/pallas_call | solution.py:316
  47.1 0.0 copy-done
  47.1 0.0 copy-done.3
  47.1 0.0 copy-done.2
  47.1 0.0 copy-start.4
  47.1 1.0 %copy-done.4 = bf16[2048,128]{1,0:T(8,128)(2,1)S(1)} copy-done((bf16[2048,128]{1,0:T(8,128)(2,1)S(1)}, bf16[2048,128]{1,0:T(8,128)(2,1)}, u32[]{:S(2)}) %copy-start.4) | copy-done | bytes 524312
  48.2 0.0 copy-start.5
  48.2 0.9 %copy-done.5 = bf16[512,128]{1,0:T(8,128)(2,1)S(1)} copy-done((bf16[512,128]{1,0:T(8,128)(2,1)S(1)}, bf16[512,128]{1,0:T(8,128)(2,1)}, u32[]{:S(2)}) %copy-start.5) | copy-done | bytes 131096
  49.1 0.0 copy-start.1
  49.1 6.5 %shard_map.103 = (bf16[64,64,128]{2,1,0:T(8,128)(2,1)S(1)}, bf16[512,128]{1,0:T(8,128)(2,1)}) custom-call(s32[22,32]{1,0:T(8,128)S(1)} %bitcast.8, s32[1,32]{1,0:T(1,128)S(1)} %bitcast.10, bf16[32,64,1408]{2,1,0:T(8,128)(2,1)S(1)} %copy-done, bf16[2048,128]{1,0:T(8,128)(2,1)S(1)} %copy-done.4, bf16[512,128]{1,0:T(8,128)(2,1)S(1)} %copy-done.5), custom_call_target="tpu_custom_call" | custom-call | flops 5905580032 | bytes 5767168 | tf_op jit(solution)/shard_map/pallas_call | solution.py:353
  55.6 0.0 copy-done.1
  55.6 11.2 %shard_map.104 = (bf16[512,128]{1,0:T(8,128)(2,1)S(1)}, f32[128,128]{1,0:T(8,128)S(1)}, f32[1,128]{1,0:T(1,128)S(1)}) custom-call(bf16[8,512,128]{2,1,0:T(8,128)(2,1)S(1)} %bitcast.6, f32[136,128]{1,0:T(8,128)S(1)} %copy-done.1), custom_call_target="tpu_custom_call" | custom-call | flops 524288 | bytes 4194304 | tf_op jit(solution)/shard_map/pallas_call | solution.py:368
  66.8 0.7 copy.14
  67.5 0.6 copy.15
  68.1 0.5 copy.16
Async XLA Ops:
  0.6 46.5 %copy-start = (bf16[32,64,1408]{2,1,0:T(8,128)(2,1)S(1)}, bf16[32,64,1408]{2,1,0:T(8,128)(2,1)}, u32[]{:S(2)}) copy-start(bf16[32,64,1408]{2,1,0:T(8,128)(2,1)} %adj_ref.1) | copy-start | bytes 17301508
  0.6 46.5 %copy-start.3 = (s32[32,1]{0,1:T(1,128)S(1)}, s32[32,1]{0,1:T(1,128)}, u32[]{:S(2)}) copy-start(s32[32,1]{0,1:T(1,128)} %param.10) | copy-start | bytes 388
  0.7 46.5 %copy-start.2 = (s32[32,22]{0,1:T(8,128)S(1)}, s32[32,22]{0,1:T(8,128)}, u32[]{:S(2)}) copy-start(s32[32,22]{0,1:T(8,128)} %param.9) | copy-start | bytes 8452
  47.1 1.0 %copy-start.4 = (bf16[2048,128]{1,0:T(8,128)(2,1)S(1)}, bf16[2048,128]{1,0:T(8,128)(2,1)}, u32[]{:S(2)}) copy-start(bf16[2048,128]{1,0:T(8,128)(2,1)} %get-tuple-element.12.grad_ref) | copy-start | bytes 1572868
  48.2 0.9 %copy-start.5 = (bf16[512,128]{1,0:T(8,128)(2,1)S(1)}, bf16[512,128]{1,0:T(8,128)(2,1)}, u32[]{:S(2)}) copy-start(bf16[512,128]{1,0:T(8,128)(2,1)} %get-tuple-element.13.act_hbm) | copy-start | bytes 393220
  49.1 6.5 %copy-start.1 = (f32[136,128]{1,0:T(8,128)S(1)}, f32[136,128]{1,0:T(8,128)}, u32[]{:S(2)}) copy-start(f32[136,128]{1,0:T(8,128)} %get-tuple-element.16.wb_ref) | copy-start | bytes 208900

commit v5 on v4

--- a/solution.py
+++ b/solution.py
@@ -41,7 +41,7 @@
 
 def forward_kernel(
     nc, nr, scale, cols_ref, counts_ref, feat_hbm, adj_hbm, weight_hbm, bias_hbm, og_hbm,
-    act_ref, grads_ref, wb_ref,
+    grads_ref, wb_ref,
     xg, adj, weight_ref, bias_ref, og_ref, own, part, rbuf, gg, w_out, w_in, w_all,
     in_sem, a_sem, f_send, f_recv, p_send, p_recv, r_send, r_recv, g_send, g_recv, w_send, w_recv, wa_send, wa_recv,
 ):
@@ -153,7 +153,7 @@
         @pl.when((r + step >= 0) & (r + step < nr))
         def start_chain(step=step):
             hop(r, step).start()
-    act_ref[...] = (preact * sig).astype(BF16)
+    grads_ref[pl.ds(nr * rows, rows), :] = (preact * sig).astype(BF16)
     feat = hidden.shape[1]
     cut = feat // nc
     w_out[:, pl.ds(0, cut), :] = scale * lax.dot_general(
@@ -203,21 +203,21 @@
     for n in range(nc):
         wb_ref[pl.ds(n * cut, cut), :] = w_all[n, pl.ds(0, cut), :]
     wb_ref[pl.ds(feat, 8), :] = w_all[0, pl.ds(cut, 8), :]
-    grads_ref[...] = gg[...].reshape(grads_ref.shape)
+    grads_ref[pl.ds(0, nr * rows), :] = gg[...].reshape(nr * rows, feat)
     for copy in row_copies + w_copies:
         copy.wait_send()
 
 
-def backward_kernel(cols_ref, counts_ref, adj_ref, grad_ref, act_hbm, out_ref, act_out, sem, *accs):
+def backward_kernel(cols_ref, counts_ref, adj_ref, grad_ref, out_ref, act_out, sem, *accs):
     blocks, tile, slot_width = adj_ref.shape
     per_row = slot_width // tile
     dead = out_ref.shape[0]
-    hand_out = pltpu.make_async_copy(act_hbm, act_out, sem)
+    hand_out = pltpu.make_async_copy(grad_ref.at[pl.ds(blocks * tile, act_out.shape[0])], act_out, sem)
     hand_out.start()
     for acc in accs:
         acc[...] = jnp.zeros_like(acc)
 
-    pace = math.gcd(blocks, 4)
+    pace = math.gcd(blocks, 8)
 
     def block_rows(n, carry):
         contribs = []
@@ -230,7 +230,7 @@
         for s in range(per_row):
             for i in range(pace):
                 b = n * pace + i
-                acc = accs[i]
+                acc = accs[i % 4]
                 j = jnp.where(s < counts_ref[0, b], cols_ref[s, b], dead)
                 acc[j] = acc[j] + contribs[i][s * tile : (s + 1) * tile]
         return carry
@@ -313,15 +313,14 @@
     dma = pltpu.SemaphoreType.DMA
     rows = blocks * tile // nr
     tile_flops = 2 * blocks * tile * slot_width * feat
-    activations, grads, wb = pl.pallas_call(
+    grads, wb = pl.pallas_call(
         functools.partial(forward_kernel, nc, nr, scale),
         out_shape=(
-            jax.ShapeDtypeStruct((rows, feat), BF16),
-            jax.ShapeDtypeStruct((blocks * tile, feat), BF16),
+            jax.ShapeDtypeStruct((blocks * tile + rows, feat), BF16),
             jax.ShapeDtypeStruct((feat + 8, feat), F32),
         ),
         in_specs=[smem, smem, hbm, hbm, hbm, hbm, hbm],
-        out_specs=(vmem, vmem, vmem),
+        out_specs=(vmem, vmem),
         scratch_shapes=[
             pltpu.VMEM((col_blocks + 1, tile, feat), BF16),
             pltpu.VMEM(adjacency.shape, BF16),
@@ -356,14 +355,14 @@
             jax.ShapeDtypeStruct((col_blocks, tile, feat), BF16),
             jax.ShapeDtypeStruct((rows, feat), BF16),
         ),
-        in_specs=[smem, smem, vmem, vmem, hbm],
+        in_specs=[smem, smem, vmem, vmem],
         out_specs=(vmem, hbm),
         scratch_shapes=[dma] + [pltpu.VMEM((col_blocks + 1, tile, feat), F32) for unused in range(4)],
         compiler_params=pltpu.CompilerParams(vmem_limit_bytes=32 * MIB),
         cost_estimate=pl.CostEstimate(
             flops=tile_flops * 8, bytes_accessed=adjacency.size * 2, transcendentals=0
         ),
-    )(tile_cols.T, row_counts.T, adjacency, grads, activations)
+    )(tile_cols.T, row_counts.T, adjacency, grads)
 
     feature_grad, weight_grad, bias_grad = pl.pallas_call(
         functools.partial(scatter_kernel, nc, nr),

time: 68.8 us -> 68.6 us (level)
  local copies, waits for them, and re-layouts: 3.75 us -> 2.89 us
  Pallas kernels: 64.1 us -> 64.8 us
    unnamed x15 -> x13, local copies, waits for them, and re-layouts: 3.75 us -> 2.89 us
where the time goes in v5:
time: 68.6 us; the launch traced here: 68.4 us
  Pallas kernels  64.8 us (94%)
  local copies, waits for them, and re-layouts  2.89 us (4%)
  between operations  0.72 us (1%)
    pallas_call x1, Pallas kernels, on_device(): pl.pallas_call(functools.partial(forward_kernel, nc, nr, scale), out_shap...  46.4 us
    pallas_call x1, Pallas kernels, on_device(): pl.pallas_call(functools.partial(scatter_kernel, nc, nr), out_shape=(jax....  11.2 us
    pallas_call x1, Pallas kernels, on_device(): pl.pallas_call(backward_kernel, out_shape=(jax.ShapeDtypeStruct((col_bloc...  7.18 us
    unnamed x13, local copies, waits for them, and re-layouts  2.89 us

profile of v5, /device:TPU:0, one launch (start us, length us, event | category | flops | bytes accessed | tf_op | source)
XLA Modules:
  0.0 68.4 jit_solution(9126479641955185746)
XLA Ops:
  0.6 0.0 copy-start
  0.6 0.0 copy-start.3
  0.7 0.0 copy-start.2
  0.7 46.4 %shard_map.102 = (bf16[2560,128]{1,0:T(8,128)(2,1)}, f32[136,128]{1,0:T(8,128)}) custom-call(s32[22,32]{1,0:T(8,128)} %bitcast.7, s32[1,32]{1,0:T(1,128)} %bitcast.9, bf16[8,64,128]{2,1,0:T(8,128)(2,1)} %bitcast.12, bf16[32,64,1408]{2,1,0:T(8,128)(2,1)} %adj_ref.1, bf16[128,128]{1,0:T(8,128)(2,1)} %weight_hbm.1, f32[1,128]{1,0:T(1,128)} %bitcast.13, ...), custom_call_target="tpu_custom_call" | custom-call | flops 738197504 | bytes 5767168 | tf_op jit(solution)/shard_map/pallas_call | solution.py:316
  47.1 0.0 copy-done
  47.1 0.0 copy-done.3
  47.1 0.0 copy-done.2
  47.1 0.0 copy-start.4
  47.1 1.1 %copy-done.4 = bf16[2560,128]{1,0:T(8,128)(2,1)S(1)} copy-done((bf16[2560,128]{1,0:T(8,128)(2,1)S(1)}, bf16[2560,128]{1,0:T(8,128)(2,1)}, u32[]{:S(2)}) %copy-start.4) | copy-done | bytes 655384
  48.2 0.0 copy-start.1
  48.2 7.2 %shard_map.103 = (bf16[64,64,128]{2,1,0:T(8,128)(2,1)S(1)}, bf16[512,128]{1,0:T(8,128)(2,1)}) custom-call(s32[22,32]{1,0:T(8,128)S(1)} %bitcast.8, s32[1,32]{1,0:T(1,128)S(1)} %bitcast.10, bf16[32,64,1408]{2,1,0:T(8,128)(2,1)S(1)} %copy-done, bf16[2560,128]{1,0:T(8,128)(2,1)S(1)} %copy-done.4), custom_call_target="tpu_custom_call" | custom-call | flops 5905580032 | bytes 5767168 | tf_op jit(solution)/shard_map/pallas_call | solution.py:352
  55.4 0.0 copy-done.1
  55.4 11.2 %shard_map.104 = (bf16[512,128]{1,0:T(8,128)(2,1)S(1)}, f32[128,128]{1,0:T(8,128)S(1)}, f32[1,128]{1,0:T(1,128)S(1)}) custom-call(bf16[8,512,128]{2,1,0:T(8,128)(2,1)S(1)} %bitcast.6, f32[136,128]{1,0:T(8,128)S(1)} %copy-done.1), custom_call_target="tpu_custom_call" | custom-call | flops 524288 | bytes 4194304 | tf_op jit(solution)/shard_map/pallas_call | solution.py:367
  66.6 0.7 copy.14
  67.3 0.6 copy.15
  67.9 0.5 copy.16
Async XLA Ops:
  0.6 46.5 %copy-start = (bf16[32,64,1408]{2,1,0:T(8,128)(2,1)S(1)}, bf16[32,64,1408]{2,1,0:T(8,128)(2,1)}, u32[]{:S(2)}) copy-start(bf16[32,64,1408]{2,1,0:T(8,128)(2,1)} %adj_ref.1) | copy-start | bytes 17301508
  0.6 46.5 %copy-start.3 = (s32[32,1]{0,1:T(1,128)S(1)}, s32[32,1]{0,1:T(1,128)}, u32[]{:S(2)}) copy-start(s32[32,1]{0,1:T(1,128)} %param.10) | copy-start | bytes 388
  0.7 46.5 %copy-start.2 = (s32[32,22]{0,1:T(8,128)S(1)}, s32[32,22]{0,1:T(8,128)}, u32[]{:S(2)}) copy-start(s32[32,22]{0,1:T(8,128)} %param.9) | copy-start | bytes 8452
  47.1 1.1 %copy-start.4 = (bf16[2560,128]{1,0:T(8,128)(2,1)S(1)}, bf16[2560,128]{1,0:T(8,128)(2,1)}, u32[]{:S(2)}) copy-start(bf16[2560,128]{1,0:T(8,128)(2,1)} %get-tuple-element.11.grad_ref) | copy-start | bytes 1966084
  48.2 7.2 %copy-start.1 = (f32[136,128]{1,0:T(8,128)S(1)}, f32[136,128]{1,0:T(8,128)}, u32[]{:S(2)}) copy-start(f32[136,128]{1,0:T(8,128)} %get-tuple-element.14.wb_ref) | copy-start | bytes 208900

commit v6 on v5

--- a/solution.py
+++ b/solution.py
@@ -217,7 +217,7 @@
     for acc in accs:
         acc[...] = jnp.zeros_like(acc)
 
-    pace = math.gcd(blocks, 8)
+    pace = math.gcd(blocks, 4)
 
     def block_rows(n, carry):
         contribs = []
@@ -230,7 +230,7 @@
         for s in range(per_row):
             for i in range(pace):
                 b = n * pace + i
-                acc = accs[i % 4]
+                acc = accs[i]
                 j = jnp.where(s < counts_ref[0, b], cols_ref[s, b], dead)
                 acc[j] = acc[j] + contribs[i][s * tile : (s + 1) * tile]
         return carry

time: 68.6 us -> 67.9 us (0.990)
  Pallas kernels: 64.8 us -> 64.1 us
where the time goes in v6:
time: 67.9 us; the launch traced here: 67.7 us
  Pallas kernels  64.1 us (94%)
  local copies, waits for them, and re-layouts  2.89 us (4%)
  between operations  0.72 us (1%)
    pallas_call x1, Pallas kernels, on_device(): pl.pallas_call(functools.partial(forward_kernel, nc, nr, scale), out_shap...  46.4 us
    pallas_call x1, Pallas kernels, on_device(): pl.pallas_call(functools.partial(scatter_kernel, nc, nr), out_shape=(jax....  11.2 us
    pallas_call x1, Pallas kernels, on_device(): pl.pallas_call(backward_kernel, out_shape=(jax.ShapeDtypeStruct((col_bloc...  6.51 us
    unnamed x13, local copies, waits for them, and re-layouts  2.89 us

profile of v6, /device:TPU:0, one launch (start us, length us, event | category | flops | bytes accessed | tf_op | source)
XLA Modules:
  0.0 67.7 jit_solution(598112378324277447)
XLA Ops:
  0.6 0.0 copy-start
  0.6 0.0 copy-start.3
  0.7 0.0 copy-start.2
  0.7 46.4 %shard_map.102 = (bf16[2560,128]{1,0:T(8,128)(2,1)}, f32[136,128]{1,0:T(8,128)}) custom-call(s32[22,32]{1,0:T(8,128)} %bitcast.7, s32[1,32]{1,0:T(1,128)} %bitcast.9, bf16[8,64,128]{2,1,0:T(8,128)(2,1)} %bitcast.12, bf16[32,64,1408]{2,1,0:T(8,128)(2,1)} %adj_ref.1, bf16[128,128]{1,0:T(8,128)(2,1)} %weight_hbm.1, f32[1,128]{1,0:T(1,128)} %bitcast.13, ...), custom_call_target="tpu_custom_call" | custom-call | flops 738197504 | bytes 5767168 | tf_op jit(solution)/shard_map/pallas_call | solution.py:316
  47.1 0.0 copy-done
  47.1 0.0 copy-done.3
  47.1 0.0 copy-done.2
  47.1 0.0 copy-start.4
  47.1 1.1 %copy-done.4 = bf16[2560,128]{1,0:T(8,128)(2,1)S(1)} copy-done((bf16[2560,128]{1,0:T(8,128)(2,1)S(1)}, bf16[2560,128]{1,0:T(8,128)(2,1)}, u32[]{:S(2)}) %copy-start.4) | copy-done | bytes 655384
  48.2 0.0 copy-start.1
  48.2 6.5 %shard_map.103 = (bf16[64,64,128]{2,1,0:T(8,128)(2,1)S(1)}, bf16[512,128]{1,0:T(8,128)(2,1)}) custom-call(s32[22,32]{1,0:T(8,128)S(1)} %bitcast.8, s32[1,32]{1,0:T(1,128)S(1)} %bitcast.10, bf16[32,64,1408]{2,1,0:T(8,128)(2,1)S(1)} %copy-done, bf16[2560,128]{1,0:T(8,128)(2,1)S(1)} %copy-done.4), custom_call_target="tpu_custom_call" | custom-call | flops 5905580032 | bytes 5767168 | tf_op jit(solution)/shard_map/pallas_call | solution.py:352
  54.7 0.0 copy-done.1
  54.7 11.2 %shard_map.104 = (bf16[512,128]{1,0:T(8,128)(2,1)S(1)}, f32[128,128]{1,0:T(8,128)S(1)}, f32[1,128]{1,0:T(1,128)S(1)}) custom-call(bf16[8,512,128]{2,1,0:T(8,128)(2,1)S(1)} %bitcast.6, f32[136,128]{1,0:T(8,128)S(1)} %copy-done.1), custom_call_target="tpu_custom_call" | custom-call | flops 524288 | bytes 4194304 | tf_op jit(solution)/shard_map/pallas_call | solution.py:367
  65.9 0.7 copy.14
  66.6 0.6 copy.15
  67.2 0.5 copy.16
Async XLA Ops:
  0.6 46.5 %copy-start = (bf16[32,64,1408]{2,1,0:T(8,128)(2,1)S(1)}, bf16[32,64,1408]{2,1,0:T(8,128)(2,1)}, u32[]{:S(2)}) copy-start(bf16[32,64,1408]{2,1,0:T(8,128)(2,1)} %adj_ref.1) | copy-start | bytes 17301508
  0.6 46.5 %copy-start.3 = (s32[32,1]{0,1:T(1,128)S(1)}, s32[32,1]{0,1:T(1,128)}, u32[]{:S(2)}) copy-start(s32[32,1]{0,1:T(1,128)} %param.10) | copy-start | bytes 388
  0.7 46.5 %copy-start.2 = (s32[32,22]{0,1:T(8,128)S(1)}, s32[32,22]{0,1:T(8,128)}, u32[]{:S(2)}) copy-start(s32[32,22]{0,1:T(8,128)} %param.9) | copy-start | bytes 8452
  47.1 1.1 %copy-start.4 = (bf16[2560,128]{1,0:T(8,128)(2,1)S(1)}, bf16[2560,128]{1,0:T(8,128)(2,1)}, u32[]{:S(2)}) copy-start(bf16[2560,128]{1,0:T(8,128)(2,1)} %get-tuple-element.11.grad_ref) | copy-start | bytes 1966084
  48.2 6.5 %copy-start.1 = (f32[136,128]{1,0:T(8,128)S(1)}, f32[136,128]{1,0:T(8,128)}, u32[]{:S(2)}) copy-start(f32[136,128]{1,0:T(8,128)} %get-tuple-element.14.wb_ref) | copy-start | bytes 208900
